TPU v7x, 32 devices: a whole 2x2x4 slice. The times are simulated.
32 devices in a mesh: groups: 2 (over x), row: 16 (over z, y, core).
Axes of the slice: x: 2, y: 2, z: 4, core: 2. Of those that a mesh axis runs over, the one named last changes fastest.
Arguments:
- tensor: float32 [256, 128, 128], P(('groups', 'row')), parts along dimension 0, may hold values from -6 to 6
- init_second: float32 [256, 512], P('groups'), parts along dimension 0, may hold values from -6 to 6
- init_third: float32 [256, 512], P('groups'), parts along dimension 0, may hold values from -6 to 6
Outputs:
- factor_first: float32 [256, 512], P(('groups', 'row')), parts along dimension 0
- factor_second: float32 [256, 512], P(('groups', 'row')), parts along dimension 0
- factor_third: float32 [256, 512], P('groups'), parts along dimension 0
- weights: float32 [1024], P('groups'), parts along dimension 0
There are 2 independent parts, one for each index of `groups`. A program takes and returns all parts, laid end to end along the dimension named above; each array names one. Nothing has to cross between parts.
All inputs are finite; a program needn't handle non-finite values.
Results may differ from a plain program's by a relative error of at most 0.0001.
Values sent between devices are 32-bit elements; how exact they have to be, the bound alone decides.
A program may use at most 128 MiB of HBM per device.

v0:
```python
import math

import jax
import jax.numpy as jnp
from jax import lax
from jax.sharding import PartitionSpec as P

HIGHEST = lax.Precision.HIGHEST
RIDGE = 0.05
EPSILON = 1e-06


def plain_gram(factor):
    return jnp.dot(factor.T, factor, precision=HIGHEST, preferred_element_type=jnp.float32)


def ridge_solve(right, first, second):
    hadamard = first * second
    shift = RIDGE * jnp.mean(jnp.diagonal(hadamard))
    system = hadamard + shift * jnp.eye(hadamard.shape[0], dtype=jnp.float32)
    lower = jnp.linalg.cholesky(system)
    return jax.scipy.linalg.cho_solve((lower, True), right.T).T


def column_scales(gram_raw):
    return jnp.sqrt(jnp.diagonal(gram_raw) + EPSILON)


def on_device(tensor, init_second, init_third):
    local_rows, second_cells, depth_cells = tensor.shape
    factor_cols = init_second.shape[1]
    devices = lax.axis_size("row")
    total_first = local_rows * devices
    gram_b0 = plain_gram(init_second) / second_cells
    gram_c0 = plain_gram(init_third) / depth_cells
    contracted = jnp.einsum("ijk,kr->ijr", tensor, init_third, precision=HIGHEST)
    right_a = jnp.einsum("ijr,jr->ir", contracted, init_second, precision=HIGHEST)
    raw_a = ridge_solve(right_a, gram_b0, gram_c0)
    gram_raw_a = lax.psum(plain_gram(raw_a), "row") / total_first
    scales_a = column_scales(gram_raw_a)
    factor_first = raw_a / scales_a
    gram_a = gram_raw_a / (scales_a[:, None] * scales_a[None, :])
    empty_product = jnp.zeros((local_rows, depth_cells, factor_cols), jnp.float32)
    segment = contracted
    right_own = lax.psum_scatter(
        jnp.einsum("ijr,ir->jr", segment, factor_first, precision=HIGHEST),
        "row",
        scatter_dimension=0,
        tiled=True,
    )
    raw_own = ridge_solve(right_own, gram_a, gram_c0)
    empty_gram = jnp.zeros((factor_cols, factor_cols), jnp.float32)
    segment = lax.all_gather(raw_own, "row", axis=0, tiled=True)
    product_raw = (empty_product, empty_gram)[0] + jnp.einsum(
        "ijk,jr->ikr", tensor, segment, precision=HIGHEST
    )
    gram_total = plain_gram(segment)
    gram_raw_b = gram_total / second_cells
    scales_b = column_scales(gram_raw_b)
    factor_second = raw_own / scales_b
    product = product_raw / scales_b
    gram_b = gram_raw_b / (scales_b[:, None] * scales_b[None, :])
    right_part = jnp.einsum("ikr,ir->kr", product, factor_first, precision=HIGHEST)
    right_c_own = lax.psum_scatter(right_part, "row", scatter_dimension=0, tiled=True)
    raw_c = lax.all_gather(ridge_solve(right_c_own, gram_a, gram_b), "row", axis=0, tiled=True)
    scales_c = jnp.sqrt(jnp.mean(raw_c * raw_c, axis=0) + EPSILON)
    factor_third = raw_c / scales_c
    weights = scales_c / math.sqrt(total_first * second_cells)
    return (factor_first, factor_second, factor_third, weights)


def solution(mesh):
    in_specs = (P(("groups", "row"), None, None), P("groups", None), P("groups", None))
    out_specs = (
        P(("groups", "row"), None),
        P(("groups", "row"), None),
        P("groups", None),
        P("groups"),
    )
    return jax.shard_map(
        on_device, mesh=mesh, in_specs=in_specs, out_specs=out_specs, check_vma=False
    )
```

profile of v0, /device:TPU:0, one launch (start us, length us, event | category | flops | bytes accessed | tf_op | source)
XLA Modules:
  0.0 632.8 jit_solution(15217960713749262886)
XLA Ops:
  7.2 2.1 convolution_multiply_fusion.1
  10.3 2.1 fusion.2
  12.4 4.7 gather_fusion
  18.5 1.3 copy.23
  19.9 1.5 fusion.5
  22.4 11.7 %cholesky.374 = f32[128,128]{1,0:T(8,128)S(1)} custom-call(f32[128,128]{1,0:T(8,128)S(1)} %cholesky.586), custom_call_target="Cholesky" | custom-call | tf_op jit(solution)/shard_map/jit(cholesky)/cholesky | solution.py:21
  34.1 9.8 %custom-call.43 = f32[1,128,128]{1,2,0:T(8,128)S(1)} custom-call(f32[1,128,128]{2,1,0:T(8,128)S(1)} %get-tuple-element.88), custom_call_target="InvertDiagBlocksLowerTriangular" | custom-call | tf_op jit(solution)/shard_map/jit(cholesky)/cholesky | solution.py:21
  46.6 11.7 %cholesky.393 = f32[128,128]{1,0:T(8,128)S(1)} custom-call(f32[128,128]{1,0:T(8,128)S(1)} %cholesky.590), custom_call_target="Cholesky" | custom-call | tf_op jit(solution)/shard_map/jit(cholesky)/cholesky | solution.py:21
  58.3 10.0 %custom-call.44 = f32[1,128,128]{1,2,0:T(8,128)S(1)} custom-call(f32[1,128,128]{2,1,0:T(8,128)S(1)} %get-tuple-element.85), custom_call_target="InvertDiagBlocksLowerTriangular" | custom-call | tf_op jit(solution)/shard_map/jit(cholesky)/cholesky | solution.py:21
  68.6 1.3 convolution_subtract_fusion.5
  69.9 11.7 %cholesky.414 = f32[128,128]{1,0:T(8,128)S(1)} custom-call(f32[128,128]{1,0:T(8,128)S(1)} %cholesky.595), custom_call_target="Cholesky" | custom-call | tf_op jit(solution)/shard_map/jit(cholesky)/cholesky | solution.py:21
  82.4 9.8 %custom-call.45 = f32[1,128,128]{1,2,0:T(8,128)S(1)} custom-call(f32[1,128,128]{2,1,0:T(8,128)S(1)} %get-tuple-element.82), custom_call_target="InvertDiagBlocksLowerTriangular" | custom-call | tf_op jit(solution)/shard_map/jit(cholesky)/cholesky | solution.py:21
  93.6 11.7 %cholesky.431 = f32[128,128]{1,0:T(8,128)S(1)} custom-call(f32[128,128]{1,0:T(8,128)S(1)} %convolution_subtract_fusion.8), custom_call_target="Cholesky" | custom-call | tf_op jit(solution)/shard_map/jit(cholesky)/cholesky | solution.py:21
  110.0 8.0 %while.6 = (s32[]{:T(128)}, f32[512,512]{1,0:T(8,128)S(1)}, s32[4,2]{0,1:T(2,128)S(1)}, f32[4,128,128]{2,1,0:T(8,128)S(1)}, s32[]{:T(128)}) while((s32[]{:T(128)}, f32[512,512]{1,0:T(8,128)S(1)}, s32[4,2]{0,1:T(2,128)S(1)}, f32[4,128,128]{2,1,0:T(8,128)S(1)}, s32[]{:T(128)}) %tuple.78), condition=%wide.while_cond, body=%wide.while_body.sunk | while | flops 2 | bytes 131189 | solution.py:22
  110.6 1.4 bitcast_dynamic-update-slice_fusion.6
  112.6 1.4 bitcast_dynamic-update-slice_fusion.6
  114.6 1.4 bitcast_dynamic-update-slice_fusion.6
  116.6 1.4 bitcast_dynamic-update-slice_fusion.6
  118.0 39.3 %custom-call.46 = f32[4,128,128]{1,2,0:T(8,128)S(1)} custom-call(f32[4,128,128]{2,1,0:T(8,128)S(1)} %get-tuple-element.26), custom_call_target="InvertDiagBlocksLowerTriangular" | custom-call | tf_op jit(solution)/shard_map/jit(_cho_solve)/triangular_solve | solution.py:22
  157.4 3.3 multiply_reduce_fusion.1
  163.5 2.0 fusion.116
  165.7 96.7 %all-reduce.3.cloned.1.call-done = f32[512,512]{0,1:T(8,128)} async-done(((f32[512,512]{0,1:T(8,128)}), f32[512,512]{0,1:T(8,128)}) %all-reduce.3.cloned.1.call-update) | async-done | bytes 1048592 | tf_op jit(solution)/shard_map/psum | solution.py:39
  262.3 1.3 broadcast_multiply_fusion
  263.7 4.5 gather_fusion.1
  268.3 2.6 multiply_reduce_fusion
  270.9 1.5 fusion.39
  272.4 4.7 gather_fusion.2
  278.4 1.3 copy.25
  279.8 1.5 fusion.4
  281.3 11.7 %cholesky.446 = f32[128,128]{1,0:T(8,128)S(1)} custom-call(f32[128,128]{1,0:T(8,128)S(1)} %cholesky.599), custom_call_target="Cholesky" | custom-call | tf_op jit(solution)/shard_map/jit(cholesky)/cholesky | solution.py:21
  293.7 9.8 %custom-call.47 = f32[1,128,128]{1,2,0:T(8,128)S(1)} custom-call(f32[1,128,128]{2,1,0:T(8,128)S(1)} %get-tuple-element.78), custom_call_target="InvertDiagBlocksLowerTriangular" | custom-call | tf_op jit(solution)/shard_map/jit(cholesky)/cholesky | solution.py:21
  304.3 11.7 %cholesky.465 = f32[128,128]{1,0:T(8,128)S(1)} custom-call(f32[128,128]{1,0:T(8,128)S(1)} %cholesky.603), custom_call_target="Cholesky" | custom-call | tf_op jit(solution)/shard_map/jit(cholesky)/cholesky | solution.py:21
  316.7 10.0 %custom-call.48 = f32[1,128,128]{1,2,0:T(8,128)S(1)} custom-call(f32[1,128,128]{2,1,0:T(8,128)S(1)} %get-tuple-element.75), custom_call_target="InvertDiagBlocksLowerTriangular" | custom-call | tf_op jit(solution)/shard_map/jit(cholesky)/cholesky | solution.py:21
  327.3 11.7 %cholesky.486 = f32[128,128]{1,0:T(8,128)S(1)} custom-call(f32[128,128]{1,0:T(8,128)S(1)} %cholesky.608), custom_call_target="Cholesky" | custom-call | tf_op jit(solution)/shard_map/jit(cholesky)/cholesky | solution.py:21
  339.8 9.8 %custom-call.49 = f32[1,128,128]{1,2,0:T(8,128)S(1)} custom-call(f32[1,128,128]{2,1,0:T(8,128)S(1)} %get-tuple-element.72), custom_call_target="InvertDiagBlocksLowerTriangular" | custom-call | tf_op jit(solution)/shard_map/jit(cholesky)/cholesky | solution.py:21
  350.2 11.7 %cholesky.503 = f32[128,128]{1,0:T(8,128)S(1)} custom-call(f32[128,128]{1,0:T(8,128)S(1)} %convolution_subtract_fusion.7), custom_call_target="Cholesky" | custom-call | tf_op jit(solution)/shard_map/jit(cholesky)/cholesky | solution.py:21
  365.5 7.7 %while.7 = (s32[]{:T(128)}, f32[512,512]{1,0:T(8,128)S(1)}, s32[4,2]{0,1:T(2,128)S(1)}, f32[4,128,128]{2,1,0:T(8,128)S(1)}, s32[]{:T(128)}) while((s32[]{:T(128)}, f32[512,512]{1,0:T(8,128)S(1)}, s32[4,2]{0,1:T(2,128)S(1)}, f32[4,128,128]{2,1,0:T(8,128)S(1)}, s32[]{:T(128)}) %tuple.93), condition=%wide.while_cond.clone, body=%wide.while_body.clone.sunk | while | flops 2 | bytes 131189 | solution.py:22
  366.1 1.3 bitcast_dynamic-update-slice_fusion.7
  368.1 1.3 bitcast_dynamic-update-slice_fusion.7
  370.0 1.3 bitcast_dynamic-update-slice_fusion.7
  371.9 1.3 bitcast_dynamic-update-slice_fusion.7
  373.4 39.3 %custom-call.50 = f32[4,128,128]{1,2,0:T(8,128)S(1)} custom-call(f32[4,128,128]{2,1,0:T(8,128)S(1)} %get-tuple-element.27), custom_call_target="InvertDiagBlocksLowerTriangular" | custom-call | tf_op jit(solution)/shard_map/jit(_cho_solve)/triangular_solve | solution.py:22
  418.3 20.2 %all_gather.6 = f32[128,512]{1,0:T(8,128)S(1)} all-gather(f32[8,512]{1,0:T(8,128)S(1)} %maximum_bitcast_fusion), channel_id=1, replica_groups=mesh['groups'=2,'row'=16] {'row'}, dimensions={0}, use_global_device_ids=true | all-gather | bytes 278528 | tf_op jit(solution)/shard_map/all_gather | solution.py:53
  439.6 4.5 gather_fusion.3
  444.1 3.2 divide_bitcast_fusion
  447.7 4.7 gather_fusion.4
  453.8 1.3 copy.28
  455.1 1.5 fusion.3
  456.6 11.7 %cholesky.518 = f32[128,128]{1,0:T(8,128)S(1)} custom-call(f32[128,128]{1,0:T(8,128)S(1)} %cholesky.612), custom_call_target="Cholesky" | custom-call | tf_op jit(solution)/shard_map/jit(cholesky)/cholesky | solution.py:21
  469.0 9.8 %custom-call.51 = f32[1,128,128]{1,2,0:T(8,128)S(1)} custom-call(f32[1,128,128]{2,1,0:T(8,128)S(1)} %get-tuple-element.68), custom_call_target="InvertDiagBlocksLowerTriangular" | custom-call | tf_op jit(solution)/shard_map/jit(cholesky)/cholesky | solution.py:21
  479.6 11.7 %cholesky.537 = f32[128,128]{1,0:T(8,128)S(1)} custom-call(f32[128,128]{1,0:T(8,128)S(1)} %cholesky.616), custom_call_target="Cholesky" | custom-call | tf_op jit(solution)/shard_map/jit(cholesky)/cholesky | solution.py:21
  492.0 10.0 %custom-call.52 = f32[1,128,128]{1,2,0:T(8,128)S(1)} custom-call(f32[1,128,128]{2,1,0:T(8,128)S(1)} %get-tuple-element.65), custom_call_target="InvertDiagBlocksLowerTriangular" | custom-call | tf_op jit(solution)/shard_map/jit(cholesky)/cholesky | solution.py:21
  502.7 11.7 %cholesky.558 = f32[128,128]{1,0:T(8,128)S(1)} custom-call(f32[128,128]{1,0:T(8,128)S(1)} %cholesky.621), custom_call_target="Cholesky" | custom-call | tf_op jit(solution)/shard_map/jit(cholesky)/cholesky | solution.py:21
  515.1 9.8 %custom-call.53 = f32[1,128,128]{1,2,0:T(8,128)S(1)} custom-call(f32[1,128,128]{2,1,0:T(8,128)S(1)} %get-tuple-element.62), custom_call_target="InvertDiagBlocksLowerTriangular" | custom-call | tf_op jit(solution)/shard_map/jit(cholesky)/cholesky | solution.py:21
  525.5 11.7 %cholesky.575 = f32[128,128]{1,0:T(8,128)S(1)} custom-call(f32[128,128]{1,0:T(8,128)S(1)} %convolution_subtract_fusion.6), custom_call_target="Cholesky" | custom-call | tf_op jit(solution)/shard_map/jit(cholesky)/cholesky | solution.py:21
  537.9 6.5 %fusion = f32[512,1,128]{2,1,0:T(1,128)S(1)} fusion(f32[8,512,1]{0,2,1:T(1,128)S(1)} %copy.47, f32[8,128,512]{1,2,0:T(8,128)} %divide_bitcast_fusion), kind=kOutput, calls=%fused_computation.11 | convolution fusion | flops 6291456 | bytes 2375680 | tf_op jit(solution)/shard_map/ikr,ir->kr/dot_general | solution.py:63
  547.9 7.7 %while.8 = (s32[]{:T(128)}, f32[512,512]{1,0:T(8,128)S(1)}, s32[4,2]{0,1:T(2,128)S(1)}, f32[4,128,128]{2,1,0:T(8,128)S(1)}, s32[]{:T(128)}) while((s32[]{:T(128)}, f32[512,512]{1,0:T(8,128)S(1)}, s32[4,2]{0,1:T(2,128)S(1)}, f32[4,128,128]{2,1,0:T(8,128)S(1)}, s32[]{:T(128)}) %tuple.94), condition=%wide.while_cond.clone.1, body=%wide.while_body.clone.1.sunk | while | flops 2 | bytes 131189 | solution.py:22
  548.5 1.3 bitcast_dynamic-update-slice_fusion.8
  550.4 1.3 bitcast_dynamic-update-slice_fusion.8
  552.3 1.3 bitcast_dynamic-update-slice_fusion.8
  554.3 1.3 bitcast_dynamic-update-slice_fusion.8
  555.6 39.3 %custom-call.54 = f32[4,128,128]{1,2,0:T(8,128)S(1)} custom-call(f32[4,128,128]{2,1,0:T(8,128)S(1)} %get-tuple-element.28), custom_call_target="InvertDiagBlocksLowerTriangular" | custom-call | tf_op jit(solution)/shard_map/jit(_cho_solve)/triangular_solve | solution.py:22
  595.5 3.2 reduce-scatter.9.cloned.1.call-done
  604.4 20.2 %all_gather.7 = f32[128,512]{1,0:T(8,128)S(1)} all-gather(f32[8,512]{1,0:T(8,128)S(1)} %maximum_bitcast_fusion.1), channel_id=1, replica_groups=mesh['groups'=2,'row'=16] {'row'}, dimensions={0}, use_global_device_ids=true | all-gather | bytes 278528 | tf_op jit(solution)/shard_map/all_gather | solution.py:65
  (169 shorter events, 47.4 us)
Async XLA Ops:
  7.2 150.2 %copy-start = (f32[8,128,128]{2,1,0:T(8,128)S(1)}, f32[8,128,128]{2,1,0:T(8,128)}, u32[]{:S(2)}) copy-start(f32[8,128,128]{2,1,0:T(8,128)} %param.6) | copy-start | bytes 1572868
  7.2 255.1 %all-reduce.3.cloned.1.call-start = ((), (), s32[]{:S(2)}) async-start(), calls=%async_computation.2 | async-start | bytes 2097152 | tf_op jit(solution)/shard_map/psum | solution.py:39
  9.4 1.0 copy-start.3
  21.3 1.0 copy-start.4
  69.9 87.5 %copy-start.5 = (f32[128,512]{1,0:T(8,128)S(1)}, f32[128,512]{1,0:T(8,128)}, u32[]{:S(2)}) copy-start(f32[128,512]{1,0:T(8,128)} %param.8) | copy-start | bytes 786436
  69.9 87.5 %copy-start.6 = (f32[128,512]{1,0:T(8,128)S(1)}, f32[128,512]{1,0:T(8,128)}, u32[]{:S(2)}) copy-start(f32[128,512]{1,0:T(8,128)} %param.7) | copy-start | bytes 786436
  165.6 247.1 %reduce-scatter.7.cloned.1.call-start = ((), (), s32[]{:S(2)}) async-start(), calls=%async_computation.3 | async-start | bytes 278528 | tf_op jit(solution)/shard_map/reduce_scatter | solution.py:45
  263.6 7.3 %copy-start.1 = (f32[512,512]{0,1:T(8,128)S(1)}, f32[512,512]{0,1:T(8,128)}, u32[]{:S(2)}) copy-start(f32[512,512]{0,1:T(8,128)} %all-reduce.3.cloned.1.call-done) | copy-start | bytes 3145732
  268.2 105.0 %copy-start.7 = (f32[512,8]{0,1:T(8,128)}, f32[512,8]{0,1:T(8,128)S(1)}, u32[]{:S(2)}) copy-start(f32[512,8]{0,1:T(8,128)S(1)} %fusion.115) | copy-start | bytes 49156
  270.9 327.9 %reduce-scatter.9.cloned.1.call-start = ((), (), s32[]{:S(2)}) async-start(), calls=%async_computation.4 | async-start | bytes 278528 | tf_op jit(solution)/shard_map/reduce_scatter | solution.py:64
  444.1 3.2 copy-start.2
Sparse Core Ops, SparseCore 0:
  165.7 96.5 all-reduce.2
  271.0 55.1 reduce-scatter.6
  545.4 53.3 reduce-scatter.8
where the time goes:
time: 636 us; the launch traced here: 633 us
  other arithmetic  371 us (58%)
  waiting for transfers between devices  100 us (16%)
  local copies, waits for them, and re-layouts  53.8 us (8%)
  matrix products  43.5 us (7%)
  blocking collectives  40.4 us (6%)
  between operations  24.2 us (4%)
    another operation x44, other arithmetic, ridge_solve(): lower = jnp.linalg.cholesky(system)  237 us
    another operation x7, other arithmetic, ridge_solve(): return jax.scipy.linalg.cho_solve((lower, True), right.T).T  119 us
    psum x1, waiting for transfers between devices, on_device(): gram_raw_a = lax.psum(plain_gram(raw_a), 'row') / total_first  96.7 us
    another operation x40, local copies, waits for them, and re-layouts, ridge_solve(): return jax.scipy.linalg.cho_solve((lower, True), right.T).T  23.2 us
    all_gather x1, blocking collectives, on_device(): lax.all_gather(ridge_solve(right_c_own, gram_a, gram_b), 'row', axis=0, t...  20.2 us
    all_gather x1, blocking collectives, on_device(): segment = lax.all_gather(raw_own, 'row', axis=0, tiled=True)  20.2 us
    gather x3, local copies, waits for them, and re-layouts, ridge_solve(): shift = RIDGE * jnp.mean(jnp.diagonal(hadamard))  14.2 us
    another operation x42, matrix products, ridge_solve(): return jax.scipy.linalg.cho_solve((lower, True), right.T).T  14.1 us
  transfers between devices with their start and end apart: 3, of which 2 were waited for; matrix products, arithmetic and copies ran while one was open for 29% of the time, Pallas kernels for 0%

commit v1 on v0

v1 whole, which is shorter than its diff:
```python
import functools
import math

import jax
import jax.numpy as jnp
from jax import lax
from jax.experimental import pallas as pl
from jax.experimental.pallas import tpu as pltpu
from jax.sharding import PartitionSpec as P

HIGHEST = lax.Precision.HIGHEST
MESH = pl.DeviceIdType.MESH
RIDGE = 0.05
EPSILON = 1e-06
SOLVE_TOL = 4e-06
MAX_ROUNDS = 2048
UNROLL = 2
VMEM_LIMIT = 56 * 1024 * 1024


def dot(a, b):
    return jnp.dot(a, b, precision=HIGHEST, preferred_element_type=jnp.float32)


def split3(value):
    high = value.astype(jnp.bfloat16).astype(jnp.float32)
    rest = value - high
    middle = rest.astype(jnp.bfloat16).astype(jnp.float32)
    return high, middle, rest - middle


def conjugate_solve(right, first, second, vh_ref, vm_ref, vl_ref):
    size = first.shape[0]
    rows = right.shape[0]
    hadamard = first * second
    eye = lax.broadcasted_iota(jnp.int32, (size, size), 0) == lax.broadcasted_iota(jnp.int32, (size, size), 1)
    diagonal = jnp.sum(jnp.where(eye, hadamard, 0.0), axis=0, keepdims=True)
    mean = jnp.sum(diagonal, axis=1, keepdims=True) / size
    inverse_mean = 1.0 / mean
    system = hadamard * inverse_mean + jnp.where(eye, RIDGE, 0.0)
    high, middle, low = split3(system)
    vh_ref[...] = high.astype(jnp.bfloat16)
    vm_ref[...] = middle.astype(jnp.bfloat16)
    vl_ref[...] = low.astype(jnp.bfloat16)
    precondition = 1.0 / (diagonal * inverse_mean + RIDGE)
    largest = jnp.max(jnp.abs(right), axis=1, keepdims=True)
    largest = jnp.where(largest > 0, largest, 1.0)

    def apply(p):
        ph, pm, plow = split3(p)
        parts = jnp.concatenate([ph, pm, plow], axis=0).astype(jnp.bfloat16)
        by_high = jnp.dot(parts, vh_ref[...], preferred_element_type=jnp.float32)
        by_middle = jnp.dot(parts, vm_ref[...], preferred_element_type=jnp.float32)
        by_low = jnp.dot(parts, vl_ref[...], preferred_element_type=jnp.float32)
        small = by_high[2 * rows :] + by_low[:rows] + by_middle[rows : 2 * rows]
        return by_high[:rows] + (by_high[rows : 2 * rows] + by_middle[:rows] + small)

    def row_sum(value):
        return jnp.sum(value, axis=1, keepdims=True)

    def one(x, r, p, rz):
        q = apply(p)
        curvature = row_sum(p * q)
        alpha = jnp.where(curvature > 0, rz / curvature, 0.0)
        x = x + alpha * p
        r = r - alpha * q
        z = r * precondition
        rz_next = row_sum(r * z)
        beta = jnp.where(rz > 0, rz_next / rz, 0.0)
        return x, r, z + beta * p, rz_next

    def body(carry):
        count, _, x, r, p, rz = carry
        for _ in range(UNROLL):
            x, r, p, rz = one(x, r, p, rz)
        excess = row_sum(r * r) - (SOLVE_TOL * RIDGE) ** 2 * row_sum(x * x)
        return count + 1, jnp.max(excess), x, r, p, rz

    def unfinished(carry):
        return jnp.logical_and(carry[1] > 0, carry[0] < MAX_ROUNDS)

    r = right / largest
    z = r * precondition
    start = (jnp.int32(0), jnp.float32(1.0), jnp.zeros_like(r), r, z, row_sum(r * z))
    x = lax.while_loop(unfinished, body, start)[2]
    return x * (largest * inverse_mean)


def first_kernel(tensor_ref, second_ref, third_ref, raw_ref, contracted_ref, gram_c_ref, vh_ref, vm_ref, vl_ref):
    second = second_ref[...]
    third = third_ref[...]
    rows = []
    for i in range(tensor_ref.shape[0]):
        contracted = dot(tensor_ref[i], third)
        contracted_ref[i] = contracted
        rows.append(jnp.sum(contracted * second, axis=0, keepdims=True))
    right = jnp.concatenate(rows, axis=0)
    gram_c = dot(third.T, third) / third.shape[0]
    gram_c_ref[...] = gram_c
    gram_b = dot(second.T, second) / second.shape[0]
    raw_ref[...] = conjugate_solve(right, gram_b, gram_c, vh_ref, vm_ref, vl_ref)


def solve_kernel(right_ref, first_ref, second_ref, raw_ref, vh_ref, vm_ref, vl_ref):
    raw_ref[...] = conjugate_solve(right_ref[...], first_ref[...], second_ref[...], vh_ref, vm_ref, vl_ref)


def greet(n):
    me = lax.axis_index("row")
    barrier = pltpu.get_barrier_semaphore()
    for step in range(1, n):
        pl.semaphore_signal(barrier, inc=1, device_id={"row": lax.rem(me + step, n)}, device_id_type=MESH)
    return me, lambda: pl.semaphore_wait(barrier, n - 1)


def gather_copies(n, me, src_ref, all_ref, send_sem, recv_sem):
    return [
        pltpu.make_async_remote_copy(
            src_ref=src_ref,
            dst_ref=all_ref.at[me],
            send_sem=send_sem.at[step],
            recv_sem=recv_sem.at[step],
            device_id={"row": lax.rem(me + step, n)},
            device_id_type=MESH,
        )
        for step in range(1, n)
    ]


def scatter_copies(n, me, part_ref, parts_ref, send_sem, recv_sem):
    return [
        pltpu.make_async_remote_copy(
            src_ref=part_ref.at[lax.rem(me + step, n)],
            dst_ref=parts_ref.at[me],
            send_sem=send_sem.at[step],
            recv_sem=recv_sem.at[step],
            device_id={"row": lax.rem(me + step, n)},
            device_id_type=MESH,
        )
        for step in range(1, n)
    ]


def gather_all(n, me, wait_barrier, raw_ref, all_ref, send_sem, recv_sem):
    copies = gather_copies(n, me, raw_ref, all_ref, send_sem, recv_sem)
    wait_barrier()
    for copy in copies:
        copy.start()
    all_ref[me] = raw_ref[...]
    return copies


def scatter_sum(n, me, right, part_ref, parts_ref, send_sem, recv_sem):
    share = right.shape[0] // n
    for device in range(n):
        part_ref[device] = right[device * share : (device + 1) * share]
    copies = scatter_copies(n, me, part_ref, parts_ref, send_sem, recv_sem)
    for copy in copies:
        copy.start()
    parts_ref[me] = part_ref[me]
    return copies


def unit_columns(all_raw):
    raw = all_raw.reshape(-1, all_raw.shape[-1])
    scales = jnp.sqrt(jnp.sum(raw * raw, axis=0, keepdims=True) / raw.shape[0] + EPSILON)
    return raw, scales


def first_exchange(
    n, raw_ref, contracted_ref, factor_ref, gram_ref, right_ref, all_ref, part_ref, parts_ref, gs, gr, ss, sr
):
    me, wait_barrier = greet(n)
    gathers = gather_all(n, me, wait_barrier, raw_ref, all_ref, gs, gr)
    for copy in gathers:
        copy.wait()
    raw, scales = unit_columns(all_ref[...])
    own = raw_ref[...] / scales
    factor_ref[...] = own
    right = contracted_ref[0] * own[0:1]
    for i in range(1, own.shape[0]):
        right = right + contracted_ref[i] * own[i : i + 1]
    scatters = scatter_sum(n, me, right, part_ref, parts_ref, ss, sr)
    factor = raw / scales
    gram_ref[...] = dot(factor.T, factor) / factor.shape[0]
    for copy in scatters:
        copy.wait()
    right_ref[...] = jnp.sum(parts_ref[...], axis=0)


def second_exchange(
    n, raw_ref, tensor_ref, first_ref, factor_ref, gram_ref, right_ref, all_ref, part_ref, parts_ref, gs, gr, ss, sr
):
    me, wait_barrier = greet(n)
    local_rows, second_cells, depth_cells = tensor_ref.shape
    turned = tensor_ref[...].reshape(local_rows * second_cells, depth_cells).T
    gathers = gather_all(n, me, wait_barrier, raw_ref, all_ref, gs, gr)
    for copy in gathers:
        copy.wait()
    raw, scales = unit_columns(all_ref[...])
    factor = raw / scales
    factor_ref[...] = raw_ref[...] / scales
    first = first_ref[...]
    pairs = jnp.concatenate([factor * first[i : i + 1] for i in range(local_rows)], axis=0)
    right = dot(turned, pairs)
    scatters = scatter_sum(n, me, right, part_ref, parts_ref, ss, sr)
    gram_ref[...] = dot(factor.T, factor) / factor.shape[0]
    for copy in scatters:
        copy.wait()
    right_ref[...] = jnp.sum(parts_ref[...], axis=0)


def third_exchange(n, total, raw_ref, factor_ref, weights_ref, all_ref, gs, gr):
    me, wait_barrier = greet(n)
    gathers = gather_all(n, me, wait_barrier, raw_ref, all_ref, gs, gr)
    for copy in gathers:
        copy.wait()
    raw = all_ref[...]
    square = jnp.sum(jnp.sum(raw * raw, axis=0), axis=0, keepdims=True)
    scales = jnp.sqrt(square / (raw.shape[0] * raw.shape[1]) + EPSILON)
    factor_ref[...] = raw / scales[None]
    weights_ref[...] = scales / math.sqrt(total)


def f32(*shape):
    return jax.ShapeDtypeStruct(shape, jnp.float32)


def call(kernel, name, out_shape, scratch, collective_id=None):
    vmem = pl.BlockSpec(memory_space=pltpu.VMEM)
    params = {} if collective_id is None else {"collective_id": collective_id, "has_side_effects": True}
    return pl.pallas_call(
        kernel,
        name=name,
        out_shape=out_shape,
        out_specs=jax.tree.map(lambda _: vmem, out_shape),
        scratch_shapes=scratch,
        compiler_params=pltpu.CompilerParams(vmem_limit_bytes=VMEM_LIMIT, **params),
    )


def on_device(tensor, init_second, init_third):
    local_rows, second_cells, depth_cells = tensor.shape
    rank = init_second.shape[1]
    n = lax.axis_size("row")
    total_first = local_rows * n
    second_own, depth_own = second_cells // n, depth_cells // n
    split = [pltpu.VMEM((rank, rank), jnp.bfloat16)] * 3
    sems = [pltpu.SemaphoreType.DMA((n,))] * 2

    def buffers(rows, shares):
        return [pltpu.VMEM((n, rows, rank), jnp.float32)] + [pltpu.VMEM((n, shares, rank), jnp.float32)] * 2

    def solve(right, first, second):
        rows = right.shape[0]
        padded = -(-rows // 8) * 8
        if padded != rows:
            right = jnp.pad(right, ((0, padded - rows), (0, 0)))
        raw = call(solve_kernel, "solve", f32(padded, rank), split)(right, first, second)
        return raw[:rows]

    raw_a, contracted, gram_c0 = call(
        first_kernel,
        "first",
        (f32(local_rows, rank), f32(local_rows, second_cells, rank), f32(rank, rank)),
        split,
    )(tensor, init_second, init_third)
    factor_first, gram_a, right_b = call(
        functools.partial(first_exchange, n),
        "first_exchange",
        (f32(local_rows, rank), f32(rank, rank), f32(second_own, rank)),
        buffers(local_rows, second_own) + sems * 2,
        0,
    )(raw_a, contracted)
    raw_b = solve(right_b, gram_a, gram_c0)
    factor_second, gram_b, right_c = call(
        functools.partial(second_exchange, n),
        "second_exchange",
        (f32(second_own, rank), f32(rank, rank), f32(depth_own, rank)),
        buffers(second_own, depth_own) + sems * 2,
        1,
    )(raw_b, tensor, factor_first)
    raw_c = solve(right_c, gram_a, gram_b)
    factor_third, weights = call(
        functools.partial(third_exchange, n, total_first * second_cells),
        "third_exchange",
        (f32(n, depth_own, rank), f32(1, rank)),
        [pltpu.VMEM((n, depth_own, rank), jnp.float32)] + sems,
        2,
    )(raw_c)
    return (factor_first, factor_second, factor_third.reshape(depth_cells, rank), weights.reshape(rank))


def solution(mesh):
    in_specs = (P(("groups", "row"), None, None), P("groups", None), P("groups", None))
    out_specs = (
        P(("groups", "row"), None),
        P(("groups", "row"), None),
        P("groups", None),
        P("groups"),
    )
    return jax.shard_map(
        on_device, mesh=mesh, in_specs=in_specs, out_specs=out_specs, check_vma=False
    )
```

time: 636 us -> 97.5 us (0.15)
  other arithmetic: 371 us -> 0 us
  waiting for transfers between devices: 100 us -> 0 us
  Pallas kernels: 0 us -> 91.4 us
  local copies, waits for them, and re-layouts: 53.8 us -> 4.12 us
  matrix products: 43.5 us -> 0 us
  blocking collectives: 40.4 us -> 0 us
  between operations: 24.2 us -> 0.68 us
    another operation x51 -> x0, other arithmetic: 356 us -> none  [the longest x44 237 us: ridge_solve(): lower = jnp.linalg.cholesky(system)]
    psum x1 -> x0, waiting for transfers between devices: 96.7 us -> none  [on_device(): gram_raw_a = lax.psum(plain_gram(raw_a), 'row') / total_first]
    pallas_call x0 -> x6, Pallas kernels: none -> 91.4 us  [the longest x1 22.4 us: on_device(): call(functools.partial(first_exchange, n), 'first_exchange', (f32(local_r...]
    all_gather x2 -> x0, blocking collectives: 40.4 us -> none  [the longest x1 20.2 us: on_device(): lax.all_gather(ridge_solve(right_c_own, gram_a, gram_b), 'row', axis=0, t...]
    another operation x52 -> x0, local copies, waits for them, and re-layouts: 23.6 us -> none  [the longest x40 23.2 us: ridge_solve(): return jax.scipy.linalg.cho_solve((lower, True), right.T).T]
    another operation x60 -> x0, matrix products: 23.3 us -> none  [the longest x42 14.1 us: ridge_solve(): return jax.scipy.linalg.cho_solve((lower, True), right.T).T]
    gather x5 -> x0, local copies, waits for them, and re-layouts: 23.3 us -> none  [the longest x3 14.2 us: ridge_solve(): shift = RIDGE * jnp.mean(jnp.diagonal(hadamard))]
    dot_general x7 -> x0, matrix products: 20.2 us -> none  [the longest x4 7.25 us: plain_gram(): jnp.dot(factor.T, factor, precision=HIGHEST, preferred_element_type=jnp.f...]
  transfers between devices with their start and end apart: 3 -> 0, of which waited for: 2 -> 0; matrix products, arithmetic and copies ran while one was open for 29% -> 0% of each run, Pallas kernels for 0% -> 0%
where the time goes in v1:
time: 97.5 us; the launch traced here: 96.2 us
  Pallas kernels  91.4 us (94%)
  local copies, waits for them, and re-layouts  4.12 us (4%)
    pallas_call x1, Pallas kernels, on_device(): call(functools.partial(first_exchange, n), 'first_exchange', (f32(local_r...  22.4 us
    pallas_call x1, Pallas kernels, on_device(): call(functools.partial(second_exchange, n), 'second_exchange', (f32(secon...  21.4 us
    pallas_call x2, Pallas kernels, solve(): call(solve_kernel, 'solve', f32(padded, rank), split)(right, first, second)  20.1 us
    pallas_call x1, Pallas kernels, on_device(): call(first_kernel, 'first', (f32(local_rows, rank), f32(local_rows, secon...  15.8 us
    pallas_call x1, Pallas kernels, on_device(): call(functools.partial(third_exchange, n, total_first * second_cells), 't...  11.7 us
    unnamed x8, local copies, waits for them, and re-layouts  4.12 us

profile of v1, /device:TPU:0, one launch (start us, length us, event | category | flops | bytes accessed | tf_op | source)
XLA Modules:
  0.0 96.2 jit_solution(5982887639011781947)
XLA Ops:
  0.6 15.8 %first.1 = (f32[8,512]{1,0:T(8,128)}, f32[8,128,512]{2,1,0:T(8,128)}, f32[512,512]{1,0:T(8,128)}) custom-call(f32[8,128,128]{2,1,0:T(8,128)} %tensor_ref.3, f32[128,512]{1,0:T(8,128)} %second_ref.1, f32[128,512]{1,0:T(8,128)} %third_ref.1), custom_call_target="tpu_custom_call" | custom-call | tf_op jit(solution)/shard_map/first/pallas_call | solution.py:262
  16.5 22.4 %first_exchange.1 = (f32[8,512]{1,0:T(8,128)}, f32[512,512]{1,0:T(8,128)}, f32[8,512]{1,0:T(8,128)}) custom-call(f32[8,512]{1,0:T(8,128)} %get-tuple-element.15.raw_ref, f32[8,128,512]{2,1,0:T(8,128)} %get-tuple-element.16.contracted_ref), custom_call_target="tpu_custom_call" | custom-call | tf_op jit(solution)/shard_map/first_exchange/pallas_call | solution.py:268
  38.9 0.0 copy-start
  38.9 10.6 %solve.2.raw_ref = f32[8,512]{1,0:T(8,128)} custom-call(f32[8,512]{1,0:T(8,128)} %get-tuple-element.18.right_ref, f32[512,512]{1,0:T(8,128)} %get-tuple-element.19.first_ref, f32[512,512]{1,0:T(8,128)} %get-tuple-element.20.second_ref), custom_call_target="tpu_custom_call" | custom-call | tf_op jit(solution)/shard_map/solve/pallas_call | solution.py:259
  49.5 21.4 %second_exchange.1 = (f32[8,512]{1,0:T(8,128)}, f32[512,512]{1,0:T(8,128)}, f32[8,512]{1,0:T(8,128)}) custom-call(f32[8,512]{1,0:T(8,128)} %solve.2.raw_ref, f32[8,128,128]{2,1,0:T(8,128)} %tensor_ref.3, f32[8,512]{1,0:T(8,128)} %get-tuple-element.30.first_ref), custom_call_target="tpu_custom_call" | custom-call | tf_op jit(solution)/shard_map/second_exchange/pallas_call | solution.py:276
  70.9 0.0 copy-start.1
  70.9 9.5 %solve.3.raw_ref = f32[8,512]{1,0:T(8,128)} custom-call(f32[8,512]{1,0:T(8,128)} %get-tuple-element.22.right_ref, f32[512,512]{1,0:T(8,128)} %get-tuple-element.19.first_ref, f32[512,512]{1,0:T(8,128)} %get-tuple-element.23.second_ref), custom_call_target="tpu_custom_call" | custom-call | tf_op jit(solution)/shard_map/solve/pallas_call | solution.py:259
  80.4 11.7 %third_exchange.1 = (f32[16,8,512]{2,1,0:T(8,128)}, f32[1,512]{1,0:T(1,128)}) custom-call(f32[8,512]{1,0:T(8,128)} %solve.3.raw_ref), custom_call_target="tpu_custom_call" | custom-call | tf_op jit(solution)/shard_map/third_exchange/pallas_call | solution.py:284
  92.1 0.0 copy-done
  92.1 0.6 copy.11
  92.7 0.0 copy-done.1
  92.7 0.6 copy.12
  93.3 1.7 %copy.13 = f32[128,512]{1,0:T(8,128)} copy(f32[128,512]{1,0:T(8,128)} %bitcast.2) | data formatting | bytes 524288
  95.0 1.2 %copy.14 = f32[512]{0:T(512)} copy(f32[512]{0:T(512)} %bitcast.3) | data formatting | bytes 4096
Async XLA Ops:
  38.9 53.2 %copy-start = (f32[8,512]{1,0:T(8,128)S(1)}, f32[8,512]{1,0:T(8,128)}, u32[]{:S(2)}) copy-start(f32[8,512]{1,0:T(8,128)} %get-tuple-element.30.first_ref) | copy-start | bytes 49156
  70.9 21.8 %copy-start.1 = (f32[8,512]{1,0:T(8,128)S(1)}, f32[8,512]{1,0:T(8,128)}, u32[]{:S(2)}) copy-start(f32[8,512]{1,0:T(8,128)} %get-tuple-element.31) | copy-start | bytes 49156

commit v2 on v1

v2 whole, which is shorter than its diff:
```python
import functools
import math

import jax
import jax.numpy as jnp
from jax import lax
from jax.experimental import pallas as pl
from jax.experimental.pallas import tpu as pltpu
from jax.sharding import PartitionSpec as P

HIGHEST = lax.Precision.HIGHEST
MESH = pl.DeviceIdType.MESH
RIDGE = 0.05
EPSILON = 1e-06
SOLVE_TOL = 4e-06
MAX_ROUNDS = 2048
UNROLL = 3
VMEM_LIMIT = 32 * 1024 * 1024


def dot(a, b):
    return jnp.dot(a, b, precision=HIGHEST, preferred_element_type=jnp.float32)


def split3(value):
    high = value.astype(jnp.bfloat16).astype(jnp.float32)
    rest = value - high
    middle = rest.astype(jnp.bfloat16).astype(jnp.float32)
    return high, middle, rest - middle


def prepare(first, second, vh_ref, vm_ref, vl_ref):
    size = first.shape[0]
    hadamard = first * second
    eye = lax.broadcasted_iota(jnp.int32, (size, size), 0) == lax.broadcasted_iota(jnp.int32, (size, size), 1)
    diagonal = jnp.sum(jnp.where(eye, hadamard, 0.0), axis=0, keepdims=True)
    mean = jnp.sum(diagonal, axis=1, keepdims=True) / size
    inverse_mean = 1.0 / mean
    system = hadamard * inverse_mean + jnp.where(eye, RIDGE, 0.0)
    high, middle, low = split3(system)
    vh_ref[...] = high.astype(jnp.bfloat16)
    vm_ref[...] = middle.astype(jnp.bfloat16)
    vl_ref[...] = low.astype(jnp.bfloat16)
    return 1.0 / (diagonal * inverse_mean + RIDGE), jnp.broadcast_to(inverse_mean, diagonal.shape)


def conjugate_solve(right, precondition, inverse_mean, vh_ref, vm_ref, vl_ref):
    rows = right.shape[0]
    largest = jnp.max(jnp.abs(right), axis=1, keepdims=True)
    largest = jnp.where(largest > 0, largest, 1.0)

    def apply(p):
        ph, pm, plow = split3(p)
        parts = jnp.concatenate([ph, pm, plow], axis=0).astype(jnp.bfloat16)
        by_high = jnp.dot(parts, vh_ref[...], preferred_element_type=jnp.float32)
        by_middle = jnp.dot(parts, vm_ref[...], preferred_element_type=jnp.float32)
        by_low = jnp.dot(parts, vl_ref[...], preferred_element_type=jnp.float32)
        small = by_high[2 * rows :] + by_low[:rows] + by_middle[rows : 2 * rows]
        return by_high[:rows] + (by_high[rows : 2 * rows] + by_middle[:rows] + small)

    def row_sum(value):
        return jnp.sum(value, axis=1, keepdims=True)

    def one(x, r, p, rz):
        q = apply(p)
        curvature = row_sum(p * q)
        alpha = jnp.where(curvature > 0, rz / curvature, 0.0)
        x = x + alpha * p
        r = r - alpha * q
        z = r * precondition
        rz_next = row_sum(r * z)
        beta = jnp.where(rz > 0, rz_next / rz, 0.0)
        return x, r, z + beta * p, rz_next

    def body(carry):
        count, _, x, r, p, rz = carry
        for _ in range(UNROLL):
            x, r, p, rz = one(x, r, p, rz)
        excess = row_sum(r * r) - (SOLVE_TOL * RIDGE) ** 2 * row_sum(x * x)
        return count + 1, jnp.max(excess), x, r, p, rz

    def unfinished(carry):
        return jnp.logical_and(carry[1] > 0, carry[0] < MAX_ROUNDS)

    r = right / largest
    z = r * precondition
    start = (jnp.int32(0), jnp.float32(1.0), jnp.zeros_like(r), r, z, row_sum(r * z))
    x = lax.while_loop(unfinished, body, start)[2]
    return x * (largest * inverse_mean)


def gram(factor):
    return dot(factor.T, factor) / factor.shape[0]


def first_kernel(tensor_ref, second_ref, third_ref, raw_ref, gram_c_ref, vh_ref, vm_ref, vl_ref):
    second = second_ref[...]
    third = third_ref[...]
    gram_c = gram(third)
    gram_c_ref[...] = gram_c
    scales = prepare(gram(second), gram_c, vh_ref, vm_ref, vl_ref)
    rows = []
    for i in range(tensor_ref.shape[0]):
        rows.append(jnp.sum(dot(tensor_ref[i], third) * second, axis=0, keepdims=True))
    raw_ref[...] = conjugate_solve(jnp.concatenate(rows, axis=0), *scales, vh_ref, vm_ref, vl_ref)


def solve_kernel(right_ref, scales_ref, vh_ref, vm_ref, vl_ref, factor_ref, raw_ref, out_ref):
    out_ref[...] = factor_ref[...]
    raw_ref[...] = conjugate_solve(right_ref[...], scales_ref[0:1], scales_ref[1:2], vh_ref, vm_ref, vl_ref)


def last_kernel(total, raw_ref, factor_ref, weights_ref):
    raw = raw_ref[...]
    square = jnp.sum(jnp.sum(raw * raw, axis=0), axis=0, keepdims=True)
    scales = jnp.sqrt(square / (raw.shape[0] * raw.shape[1]) + EPSILON)
    factor_ref[...] = raw / scales[None]
    weights_ref[...] = scales / math.sqrt(total)


class Place:
    def __init__(self, n):
        self.n = n
        self.chips = n // 2
        self.me = lax.axis_index("row")
        self.chip = self.me // 2
        self.core = lax.rem(self.me, 2)
        self.partner = self.chip * 2 + 1 - self.core

    def chip_after(self, step):
        return lax.rem(self.chip + step, self.chips)

    def chip_before(self, step):
        return lax.rem(self.chip + self.chips - step, self.chips)

    def greet(self):
        barrier = pltpu.get_barrier_semaphore()
        for step in range(1, self.n):
            device = {"row": lax.rem(self.me + step, self.n)}
            pl.semaphore_signal(barrier, inc=1, device_id=device, device_id_type=MESH)
        return barrier

    def send(self, src, dst, sems, at, device):
        return pltpu.make_async_remote_copy(
            src_ref=src,
            dst_ref=dst,
            send_sem=sems.at[0, at],
            recv_sem=sems.at[1, at],
            device_id={"row": device},
            device_id_type=MESH,
        )


def gather_start(place, raw_ref, all_ref, sems):
    own = all_ref.at[place.me]
    copies = []
    for step in range(1, place.chips):
        device = place.chip_after(step) * 2 + place.core
        copies.append(place.send(raw_ref, own, sems, step, device))
    copies.append(place.send(raw_ref, own, sems, 0, place.partner))
    for copy in copies:
        copy.start()
    all_ref[place.me] = raw_ref[...]
    return copies


def gather_finish(place, copies, all_ref, sems):
    forwards = []
    for step in range(1, place.chips):
        copies[step - 1].wait_recv()
        slot = all_ref.at[place.chip_before(step) * 2 + place.core]
        forward = place.send(slot, slot, sems, step, place.partner)
        forward.start()
        forwards.append(forward)
    copies[-1].wait_recv()
    for forward in forwards:
        forward.wait_recv()
    return copies + forwards


def split_parts(place, right, part_ref):
    share = right.shape[0] // place.n
    for device in range(place.n):
        part_ref[device % 2, device // 2] = right[device * share : (device + 1) * share]


def pair_start(place, part_ref, pair_ref, sems):
    copy = place.send(part_ref.at[1 - place.core], pair_ref, sems, 0, place.partner)
    copy.start()
    return copy


def scatter_start(place, pair_copy, part_ref, pair_ref, parts_ref, sems):
    pair_copy.wait()
    part_ref[place.core] = part_ref[place.core] + pair_ref[...]
    copies = []
    for step in range(1, place.chips):
        chip = place.chip_after(step)
        copy = place.send(
            part_ref.at[place.core, chip], parts_ref.at[place.chip], sems, step, chip * 2 + place.core
        )
        copy.start()
        copies.append(copy)
    parts_ref[place.chip] = part_ref[place.core, place.chip]
    return copies


def scatter_finish(copies, parts_ref):
    for copy in copies:
        copy.wait_recv()
    return jnp.sum(parts_ref[...], axis=0)


def unit_columns(all_raw):
    raw = all_raw.reshape(-1, all_raw.shape[-1])
    scales = jnp.sqrt(jnp.sum(raw * raw, axis=0, keepdims=True) / raw.shape[0] + EPSILON)
    return raw / scales, scales


def first_exchange(
    n, raw_ref, tensor_ref, third_ref, gram_c_ref, factor_ref, gram_ref, right_ref, scales_ref, vh_ref, vm_ref, vl_ref,
    all_ref, part_ref, pair_ref, parts_ref, gather_sems, forward_sems, scatter_sems
):
    place = Place(n)
    barrier = place.greet()
    raw = raw_ref[...]
    local_rows = tensor_ref.shape[0]
    slabs = jnp.concatenate([tensor_ref[i] for i in range(local_rows)], axis=1)
    third = third_ref[...]
    pairs = jnp.concatenate([third * raw[i : i + 1] for i in range(local_rows)], axis=0)
    split_parts(place, dot(slabs, pairs), part_ref)
    pl.semaphore_wait(barrier, n - 1)
    pair_copy = pair_start(place, part_ref, pair_ref, scatter_sems)
    gathers = gather_start(place, raw_ref, all_ref, gather_sems)
    scatters = scatter_start(place, pair_copy, part_ref, pair_ref, parts_ref, scatter_sems)
    gathers = gather_finish(place, gathers, all_ref, forward_sems)
    factor, scales = unit_columns(all_ref[...])
    factor_ref[...] = raw / scales
    gram_a = gram(factor)
    gram_ref[...] = gram_a
    scales_ref[0:1], scales_ref[1:2] = prepare(gram_a, gram_c_ref[...], vh_ref, vm_ref, vl_ref)
    right_ref[...] = scatter_finish(scatters, parts_ref) / scales
    for copy in gathers + scatters:
        copy.wait_send()


def second_exchange(
    n, raw_ref, tensor_ref, first_ref, gram_a_ref, factor_ref, right_ref, scales_ref, vh_ref, vm_ref, vl_ref,
    all_ref, part_ref, pair_ref, parts_ref, gather_sems, forward_sems, scatter_sems
):
    place = Place(n)
    barrier = place.greet()
    local_rows, second_cells, depth_cells = tensor_ref.shape
    turned = tensor_ref[...].reshape(local_rows * second_cells, depth_cells).T
    pl.semaphore_wait(barrier, n - 1)
    gathers = gather_start(place, raw_ref, all_ref, gather_sems)
    gathers = gather_finish(place, gathers, all_ref, forward_sems)
    factor, scales = unit_columns(all_ref[...])
    factor_ref[...] = raw_ref[...] / scales
    first = first_ref[...]
    pairs = jnp.concatenate([factor * first[i : i + 1] for i in range(local_rows)], axis=0)
    split_parts(place, dot(turned, pairs), part_ref)
    pair_copy = pair_start(place, part_ref, pair_ref, scatter_sems)
    gram_b = gram(factor)
    scatters = scatter_start(place, pair_copy, part_ref, pair_ref, parts_ref, scatter_sems)
    scales_ref[0:1], scales_ref[1:2] = prepare(gram_a_ref[...], gram_b, vh_ref, vm_ref, vl_ref)
    right_ref[...] = scatter_finish(scatters, parts_ref)
    for copy in gathers + scatters:
        copy.wait_send()


def third_exchange(n, raw_ref, all_out_ref, all_ref, gather_sems, forward_sems):
    place = Place(n)
    barrier = place.greet()
    pl.semaphore_wait(barrier, n - 1)
    gathers = gather_start(place, raw_ref, all_ref, gather_sems)
    gathers = gather_finish(place, gathers, all_ref, forward_sems)
    all_out_ref[...] = all_ref[...]
    for copy in gathers:
        copy.wait_send()


def f32(*shape):
    return jax.ShapeDtypeStruct(shape, jnp.float32)


def call(kernel, name, out_shape, scratch, collective_id=None):
    vmem = pl.BlockSpec(memory_space=pltpu.VMEM)
    params = {} if collective_id is None else {"collective_id": collective_id, "has_side_effects": True}
    return pl.pallas_call(
        kernel,
        name=name,
        out_shape=out_shape,
        out_specs=jax.tree.map(lambda _: vmem, out_shape),
        scratch_shapes=scratch,
        compiler_params=pltpu.CompilerParams(vmem_limit_bytes=VMEM_LIMIT, **params),
    )


def on_device(tensor, init_second, init_third):
    local_rows, second_cells, depth_cells = tensor.shape
    rank = init_second.shape[1]
    n = lax.axis_size("row")
    chips = n // 2
    second_own, depth_own = second_cells // n, depth_cells // n
    system = [jax.ShapeDtypeStruct((rank, rank), jnp.bfloat16)] * 3
    split = [pltpu.VMEM((rank, rank), jnp.bfloat16)] * 3
    gather_sems = pltpu.SemaphoreType.DMA((2, chips))

    def buffers(rows, share):
        return [
            pltpu.VMEM((n, rows, rank), jnp.float32),
            pltpu.VMEM((2, chips, share, rank), jnp.float32),
            pltpu.VMEM((chips, share, rank), jnp.float32),
            pltpu.VMEM((chips, share, rank), jnp.float32),
            gather_sems,
            gather_sems,
            gather_sems,
        ]

    def solve(right, scales, parts, factor):
        rows = right.shape[0]
        padded = -(-rows // 8) * 8
        if padded != rows:
            right = jnp.pad(right, ((0, padded - rows), (0, 0)))
        raw, out = call(solve_kernel, "solve", (f32(padded, rank), f32(*factor.shape)), [])(
            right, scales, *parts, factor
        )
        return raw[:rows], out

    raw_a, gram_c0 = call(first_kernel, "first", (f32(local_rows, rank), f32(rank, rank)), split)(
        tensor, init_second, init_third
    )
    factor_first, gram_a, right_b, scales_b, *parts_b = call(
        functools.partial(first_exchange, n),
        "first_exchange",
        (f32(local_rows, rank), f32(rank, rank), f32(second_own, rank), f32(2, rank), *system),
        buffers(local_rows, second_own),
        0,
    )(raw_a, tensor, init_third, gram_c0)
    raw_b, factor_first_out = solve(right_b, scales_b, parts_b, factor_first)
    factor_second, right_c, scales_c, *parts_c = call(
        functools.partial(second_exchange, n),
        "second_exchange",
        (f32(second_own, rank), f32(depth_own, rank), f32(2, rank), *system),
        buffers(second_own, depth_own),
        1,
    )(raw_b, tensor, factor_first, gram_a)
    raw_c, factor_second_out = solve(right_c, scales_c, parts_c, factor_second)
    all_c = call(
        functools.partial(third_exchange, n),
        "third_exchange",
        f32(n, depth_own, rank),
        [pltpu.VMEM((n, depth_own, rank), jnp.float32), gather_sems, gather_sems],
        2,
    )(raw_c)
    factor_third, weights = call(
        functools.partial(last_kernel, local_rows * n * second_cells),
        "last",
        (f32(n, depth_own, rank), f32(1, rank)),
        [],
    )(all_c)
    return (
        factor_first_out,
        factor_second_out,
        factor_third.reshape(depth_cells, rank),
        weights.reshape(rank),
    )


def solution(mesh):
    in_specs = (P(("groups", "row"), None, None), P("groups", None), P("groups", None))
    out_specs = (
        P(("groups", "row"), None),
        P(("groups", "row"), None),
        P("groups", None),
        P("groups"),
    )
    return jax.shard_map(
        on_device, mesh=mesh, in_specs=in_specs, out_specs=out_specs, check_vma=False
    )
```

time: 97.5 us -> 74.6 us (0.77); the launches traced: 96.2 us -> 74.4 us
  Pallas kernels: 91.4 us -> 70.7 us
  local copies, waits for them, and re-layouts: 4.12 us -> 2.95 us
    pallas_call x1, Pallas kernels: 22.4 us -> 13.2 us  [on_device(): call(functools.partial(first_exchange, n), 'first_exchange', (f32(local_r...]
    pallas_call x4 -> x5, Pallas kernels: 47.7 us -> 39 us  [the longest x2 16.2 us: solve(): call(solve_kernel, 'solve', (f32(padded, rank), f32(*factor.shape)), [])]
    pallas_call x1, Pallas kernels: 21.4 us -> 18.5 us  [on_device(): call(functools.partial(second_exchange, n), 'second_exchange', (f32(secon...]
    unnamed x8 -> x10, local copies, waits for them, and re-layouts: 4.12 us -> 2.95 us
where the time goes in v2:
time: 74.6 us; the launch traced here: 74.4 us
  Pallas kernels  70.7 us (95%)
  local copies, waits for them, and re-layouts  2.95 us (4%)
    pallas_call x1, Pallas kernels, on_device(): call(functools.partial(second_exchange, n), 'second_exchange', (f32(secon...  18.5 us
    pallas_call x2, Pallas kernels, solve(): call(solve_kernel, 'solve', (f32(padded, rank), f32(*factor.shape)), [])  16.2 us
    pallas_call x1, Pallas kernels, on_device(): call(first_kernel, 'first', (f32(local_rows, rank), f32(rank, rank)), split)  14.1 us
    pallas_call x1, Pallas kernels, on_device(): call(functools.partial(first_exchange, n), 'first_exchange', (f32(local_r...  13.2 us
    pallas_call x1, Pallas kernels, on_device(): call(functools.partial(third_exchange, n), 'third_exchange', f32(n, depth...  7.92 us
    unnamed x10, local copies, waits for them, and re-layouts  2.95 us

profile of v2, /device:TPU:0, one launch (start us, length us, event | category | flops | bytes accessed | tf_op | source)
XLA Modules:
  0.0 74.4 jit_solution(5054829450224241913)
XLA Ops:
  0.6 0.0 copy-start
  0.6 1.0 %copy-done = f32[8,128,128]{2,1,0:T(8,128)S(1)} copy-done((f32[8,128,128]{2,1,0:T(8,128)S(1)}, f32[8,128,128]{2,1,0:T(8,128)}, u32[]{:S(2)}) %copy-start) | copy-done | bytes 524312
  1.7 0.0 copy-start.2
  1.7 0.9 %copy-done.2 = f32[128,512]{1,0:T(8,128)S(1)} copy-done((f32[128,512]{1,0:T(8,128)S(1)}, f32[128,512]{1,0:T(8,128)}, u32[]{:S(2)}) %copy-start.2) | copy-done | bytes 262168
  2.6 0.0 copy-start.4
  2.6 0.9 %copy-done.4 = f32[128,512]{1,0:T(8,128)S(1)} copy-done((f32[128,512]{1,0:T(8,128)S(1)}, f32[128,512]{1,0:T(8,128)}, u32[]{:S(2)}) %copy-start.4) | copy-done | bytes 262168
  3.6 0.0 copy-start.3
  3.6 14.1 %first.1 = (f32[8,512]{1,0:T(8,128)S(1)}, f32[512,512]{1,0:T(8,128)S(1)}) custom-call(f32[8,128,128]{2,1,0:T(8,128)S(1)} %copy-done, f32[128,512]{1,0:T(8,128)S(1)} %copy-done.4, f32[128,512]{1,0:T(8,128)S(1)} %copy-done.2), custom_call_target="tpu_custom_call" | custom-call | tf_op jit(solution)/shard_map/first/pallas_call | solution.py:331
  17.7 0.0 copy-done.3
  17.7 13.2 %first_exchange.1 = (f32[8,512]{1,0:T(8,128)S(1)}, f32[512,512]{1,0:T(8,128)S(1)}, f32[8,512]{1,0:T(8,128)S(1)}, f32[2,512]{1,0:T(2,128)S(1)}, bf16[512,512]{1,0...) custom-call(f32[8,512]{1,0:T(8,128)S(1)} %get-tuple-element.25.raw_ref, ...), custom_call_target="tpu_custom_call" | custom-call | tf_op jit(solution)/shard_map/first_exchange/pallas_call | solution.py:334
  31.0 0.0 copy-start.1
  31.0 8.9 %solve.2 = (f32[8,512]{1,0:T(8,128)S(1)}, f32[8,512]{1,0:T(8,128)}) custom-call(f32[8,512]{1,0:T(8,128)S(1)} %get-tuple-element.27.right_ref, f32[2,512]{1,0:T(2,128)S(1)} %get-tuple-element.28.scales_ref, bf16[512,512]{1,0:T(8,128)(2,1)S(1)} %get-tuple-element.29.vh_ref, bf16[512,512]{1,0:T(8,128)(2,1)S(1)} %get-tuple-element.30.vm_ref, ...), custom_call_target="tpu_custom_call" | custom-call | tf_op jit(solution)/shard_map/solve/pallas_call | solution.py:326
  39.9 0.0 copy-done.1
  39.9 18.5 %second_exchange.1 = (f32[8,512]{1,0:T(8,128)S(1)}, f32[8,512]{1,0:T(8,128)S(1)}, f32[2,512]{1,0:T(2,128)S(1)}, bf16[512,512]{1,0:T(8,128)(2,1)S(1)}, bf16[512,5...) custom-call(f32[8,512]{1,0:T(8,128)S(1)} %get-tuple-element.34.raw_ref, f32[8,128,128]{2,1,0:T(8,128)S(1)} %copy-done.1, ...), custom_call_target="tpu_custom_call" | custom-call | tf_op jit(solution)/shard_map/second_exchange/pallas_call | solution.py:342
  58.4 7.3 %solve.3 = (f32[8,512]{1,0:T(8,128)S(1)}, f32[8,512]{1,0:T(8,128)}) custom-call(f32[8,512]{1,0:T(8,128)S(1)} %get-tuple-element.36.right_ref, f32[2,512]{1,0:T(2,128)S(1)} %get-tuple-element.37.scales_ref, bf16[512,512]{1,0:T(8,128)(2,1)S(1)} %get-tuple-element.38.vh_ref, bf16[512,512]{1,0:T(8,128)(2,1)S(1)} %get-tuple-element.39.vm_ref, ...), custom_call_target="tpu_custom_call" | custom-call | tf_op jit(solution)/shard_map/solve/pallas_call | solution.py:326
  65.7 7.9 %third_exchange.1.raw_ref = f32[16,8,512]{2,1,0:T(8,128)S(1)} custom-call(f32[8,512]{1,0:T(8,128)S(1)} %get-tuple-element.43.raw_ref), custom_call_target="tpu_custom_call" | custom-call | tf_op jit(solution)/shard_map/third_exchange/pallas_call | solution.py:350
  73.6 0.8 %last.1 = (f32[16,8,512]{2,1,0:T(8,128)}, f32[1,512]{1,0:T(1,128)}) custom-call(f32[16,8,512]{2,1,0:T(8,128)S(1)} %third_exchange.1.raw_ref), custom_call_target="tpu_custom_call" | custom-call | tf_op jit(solution)/shard_map/last/pallas_call | solution.py:357
Async XLA Ops:
  0.6 1.0 %copy-start = (f32[8,128,128]{2,1,0:T(8,128)S(1)}, f32[8,128,128]{2,1,0:T(8,128)}, u32[]{:S(2)}) copy-start(f32[8,128,128]{2,1,0:T(8,128)} %tensor_ref.5) | copy-start | bytes 1572868
  1.7 0.9 %copy-start.2 = (f32[128,512]{1,0:T(8,128)S(1)}, f32[128,512]{1,0:T(8,128)}, u32[]{:S(2)}) copy-start(f32[128,512]{1,0:T(8,128)} %third_ref.3) | copy-start | bytes 786436
  2.6 0.9 %copy-start.4 = (f32[128,512]{1,0:T(8,128)S(1)}, f32[128,512]{1,0:T(8,128)}, u32[]{:S(2)}) copy-start(f32[128,512]{1,0:T(8,128)} %second_ref.1) | copy-start | bytes 786436
  3.6 14.1 %copy-start.3 = (f32[128,512]{1,0:T(8,128)S(1)}, f32[128,512]{1,0:T(8,128)}, u32[]{:S(2)}) copy-start(f32[128,512]{1,0:T(8,128)} %third_ref.3) | copy-start | bytes 786436
  31.0 8.9 %copy-start.1 = (f32[8,128,128]{2,1,0:T(8,128)S(1)}, f32[8,128,128]{2,1,0:T(8,128)}, u32[]{:S(2)}) copy-start(f32[8,128,128]{2,1,0:T(8,128)} %tensor_ref.5) | copy-start | bytes 1572868

commit v3 on v2

--- a/solution.py
+++ b/solution.py
@@ -15,7 +15,8 @@
 SOLVE_TOL = 4e-06
 MAX_ROUNDS = 2048
 UNROLL = 3
-VMEM_LIMIT = 32 * 1024 * 1024
+VMEM_LIMIT = 40 * 1024 * 1024
+FIRST_LIMIT = 63 * 1024 * 1024
 
 
 def dot(a, b):
@@ -93,12 +94,24 @@
     return dot(factor.T, factor) / factor.shape[0]
 
 
-def first_kernel(tensor_ref, second_ref, third_ref, raw_ref, gram_c_ref, vh_ref, vm_ref, vl_ref):
-    second = second_ref[...]
+def first_kernel(
+    tensor_hbm, second_hbm, third_hbm, raw_ref, vh_ref, vm_ref, vl_ref, tensor_ref, second_ref, third_ref, sems
+):
+    loads = [
+        pltpu.make_async_copy(source, target, sems.at[at])
+        for at, (source, target) in enumerate(
+            ((third_hbm, third_ref), (second_hbm, second_ref), (tensor_hbm, tensor_ref))
+        )
+    ]
+    for load in loads:
+        load.start()
+    loads[0].wait()
     third = third_ref[...]
     gram_c = gram(third)
-    gram_c_ref[...] = gram_c
+    loads[1].wait()
+    second = second_ref[...]
     scales = prepare(gram(second), gram_c, vh_ref, vm_ref, vl_ref)
+    loads[2].wait()
     rows = []
     for i in range(tensor_ref.shape[0]):
         rows.append(jnp.sum(dot(tensor_ref[i], third) * second, axis=0, keepdims=True))
@@ -135,10 +148,11 @@
 
     def greet(self):
         barrier = pltpu.get_barrier_semaphore()
-        for step in range(1, self.n):
-            device = {"row": lax.rem(self.me + step, self.n)}
+        for step in range(1, self.chips):
+            device = {"row": self.chip_after(step) * 2 + self.core}
             pl.semaphore_signal(barrier, inc=1, device_id=device, device_id_type=MESH)
-        return barrier
+        pl.semaphore_signal(barrier, inc=1, device_id={"row": self.partner}, device_id_type=MESH)
+        return lambda: pl.semaphore_wait(barrier, self.chips)
 
     def send(self, src, dst, sems, at, device):
         return pltpu.make_async_remote_copy(
@@ -217,62 +231,54 @@
     return raw / scales, scales
 
 
-def first_exchange(
-    n, raw_ref, tensor_ref, third_ref, gram_c_ref, factor_ref, gram_ref, right_ref, scales_ref, vh_ref, vm_ref, vl_ref,
-    all_ref, part_ref, pair_ref, parts_ref, gather_sems, forward_sems, scatter_sems
-):
+def exchange(place, wait_barrier, terms, other_gram, raw_ref, right_ref, scales_ref, vh_ref, vm_ref, vl_ref,
+             all_ref, part_ref, pair_ref, parts_ref, gather_sems, forward_sems, scatter_sems):
+    split_parts(place, terms, part_ref)
+    wait_barrier()
+    pair_copy = pair_start(place, part_ref, pair_ref, scatter_sems)
+    gathers = gather_start(place, raw_ref, all_ref, gather_sems)
+    scatters = scatter_start(place, pair_copy, part_ref, pair_ref, parts_ref, scatter_sems)
+    gathers = gather_finish(place, gathers, all_ref, forward_sems)
+    factor, scales = unit_columns(all_ref[...])
+    own_gram = gram(factor)
+    scales_ref[0:1], scales_ref[1:2] = prepare(own_gram, other_gram, vh_ref, vm_ref, vl_ref)
+    right_ref[...] = scatter_finish(scatters, parts_ref) / scales
+    for copy in gathers + scatters:
+        copy.wait_send()
+    return factor, own_gram, scales
+
+
+def first_exchange(n, raw_ref, tensor_ref, third_ref, factor_ref, all_factor_ref, gram_ref, *refs):
     place = Place(n)
-    barrier = place.greet()
+    wait_barrier = place.greet()
     raw = raw_ref[...]
     local_rows = tensor_ref.shape[0]
     slabs = jnp.concatenate([tensor_ref[i] for i in range(local_rows)], axis=1)
     third = third_ref[...]
     pairs = jnp.concatenate([third * raw[i : i + 1] for i in range(local_rows)], axis=0)
-    split_parts(place, dot(slabs, pairs), part_ref)
-    pl.semaphore_wait(barrier, n - 1)
-    pair_copy = pair_start(place, part_ref, pair_ref, scatter_sems)
-    gathers = gather_start(place, raw_ref, all_ref, gather_sems)
-    scatters = scatter_start(place, pair_copy, part_ref, pair_ref, parts_ref, scatter_sems)
-    gathers = gather_finish(place, gathers, all_ref, forward_sems)
-    factor, scales = unit_columns(all_ref[...])
+    terms = dot(slabs, pairs)
+    factor, gram_a, scales = exchange(place, wait_barrier, terms, gram(third), raw_ref, *refs)
+    all_factor_ref[...] = factor
+    gram_ref[...] = gram_a
     factor_ref[...] = raw / scales
-    gram_a = gram(factor)
-    gram_ref[...] = gram_a
-    scales_ref[0:1], scales_ref[1:2] = prepare(gram_a, gram_c_ref[...], vh_ref, vm_ref, vl_ref)
-    right_ref[...] = scatter_finish(scatters, parts_ref) / scales
-    for copy in gathers + scatters:
-        copy.wait_send()
-
-
-def second_exchange(
-    n, raw_ref, tensor_ref, first_ref, gram_a_ref, factor_ref, right_ref, scales_ref, vh_ref, vm_ref, vl_ref,
-    all_ref, part_ref, pair_ref, parts_ref, gather_sems, forward_sems, scatter_sems
-):
+
+
+def second_exchange(n, raw_ref, swapped_ref, first_ref, gram_a_ref, factor_ref, *refs):
     place = Place(n)
-    barrier = place.greet()
-    local_rows, second_cells, depth_cells = tensor_ref.shape
-    turned = tensor_ref[...].reshape(local_rows * second_cells, depth_cells).T
-    pl.semaphore_wait(barrier, n - 1)
-    gathers = gather_start(place, raw_ref, all_ref, gather_sems)
-    gathers = gather_finish(place, gathers, all_ref, forward_sems)
-    factor, scales = unit_columns(all_ref[...])
-    factor_ref[...] = raw_ref[...] / scales
+    wait_barrier = place.greet()
+    raw = raw_ref[...]
+    turned = swapped_ref[...].reshape(-1, swapped_ref.shape[-1]).T
     first = first_ref[...]
-    pairs = jnp.concatenate([factor * first[i : i + 1] for i in range(local_rows)], axis=0)
-    split_parts(place, dot(turned, pairs), part_ref)
-    pair_copy = pair_start(place, part_ref, pair_ref, scatter_sems)
-    gram_b = gram(factor)
-    scatters = scatter_start(place, pair_copy, part_ref, pair_ref, parts_ref, scatter_sems)
-    scales_ref[0:1], scales_ref[1:2] = prepare(gram_a_ref[...], gram_b, vh_ref, vm_ref, vl_ref)
-    right_ref[...] = scatter_finish(scatters, parts_ref)
-    for copy in gathers + scatters:
-        copy.wait_send()
+    pairs = jnp.concatenate([raw * first[i : i + 1] for i in range(first.shape[0])], axis=0)
+    terms = dot(turned, pairs)
+    _, _, scales = exchange(place, wait_barrier, terms, gram_a_ref[...], raw_ref, *refs)
+    factor_ref[...] = raw / scales
 
 
 def third_exchange(n, raw_ref, all_out_ref, all_ref, gather_sems, forward_sems):
     place = Place(n)
-    barrier = place.greet()
-    pl.semaphore_wait(barrier, n - 1)
+    wait_barrier = place.greet()
+    wait_barrier()
     gathers = gather_start(place, raw_ref, all_ref, gather_sems)
     gathers = gather_finish(place, gathers, all_ref, forward_sems)
     all_out_ref[...] = all_ref[...]
@@ -284,16 +290,17 @@
     return jax.ShapeDtypeStruct(shape, jnp.float32)
 
 
-def call(kernel, name, out_shape, scratch, collective_id=None):
+def call(kernel, name, out_shape, scratch, collective_id=None, in_specs=None, limit=VMEM_LIMIT):
     vmem = pl.BlockSpec(memory_space=pltpu.VMEM)
     params = {} if collective_id is None else {"collective_id": collective_id, "has_side_effects": True}
     return pl.pallas_call(
         kernel,
         name=name,
         out_shape=out_shape,
+        **({} if in_specs is None else {"in_specs": in_specs}),
         out_specs=jax.tree.map(lambda _: vmem, out_shape),
         scratch_shapes=scratch,
-        compiler_params=pltpu.CompilerParams(vmem_limit_bytes=VMEM_LIMIT, **params),
+        compiler_params=pltpu.CompilerParams(vmem_limit_bytes=limit, **params),
     )
 
 
@@ -302,6 +309,7 @@
     rank = init_second.shape[1]
     n = lax.axis_size("row")
     chips = n // 2
+    total_first = local_rows * n
     second_own, depth_own = second_cells // n, depth_cells // n
     system = [jax.ShapeDtypeStruct((rank, rank), jnp.bfloat16)] * 3
     split = [pltpu.VMEM((rank, rank), jnp.bfloat16)] * 3
@@ -328,16 +336,24 @@
         )
         return raw[:rows], out
 
-    raw_a, gram_c0 = call(first_kernel, "first", (f32(local_rows, rank), f32(rank, rank)), split)(
-        tensor, init_second, init_third
-    )
-    factor_first, gram_a, right_b, scales_b, *parts_b = call(
+    blocks = tensor.reshape(local_rows, n, second_own, depth_cells).transpose(1, 0, 2, 3)
+    swapped = lax.all_to_all(blocks, "row", 0, 0, tiled=True)
+    staged = [pltpu.VMEM(whole.shape, jnp.float32) for whole in (tensor, init_second, init_third)]
+    raw_a = call(
+        first_kernel,
+        "first",
+        f32(local_rows, rank),
+        split + staged + [pltpu.SemaphoreType.DMA((3,))],
+        in_specs=[pl.BlockSpec(memory_space=pltpu.HBM)] * 3,
+        limit=FIRST_LIMIT,
+    )(tensor, init_second, init_third)
+    factor_first, all_first, gram_a, right_b, scales_b, *parts_b = call(
         functools.partial(first_exchange, n),
         "first_exchange",
-        (f32(local_rows, rank), f32(rank, rank), f32(second_own, rank), f32(2, rank), *system),
+        (f32(local_rows, rank), f32(total_first, rank), f32(rank, rank), f32(second_own, rank), f32(2, rank), *system),
         buffers(local_rows, second_own),
         0,
-    )(raw_a, tensor, init_third, gram_c0)
+    )(raw_a, tensor, init_third)
     raw_b, factor_first_out = solve(right_b, scales_b, parts_b, factor_first)
     factor_second, right_c, scales_c, *parts_c = call(
         functools.partial(second_exchange, n),
@@ -345,7 +361,7 @@
         (f32(second_own, rank), f32(depth_own, rank), f32(2, rank), *system),
         buffers(second_own, depth_own),
         1,
-    )(raw_b, tensor, factor_first, gram_a)
+    )(raw_b, swapped, all_first, gram_a)
     raw_c, factor_second_out = solve(right_c, scales_c, parts_c, factor_second)
     all_c = call(
         functools.partial(third_exchange, n),
@@ -355,7 +371,7 @@
         2,
     )(raw_c)
     factor_third, weights = call(
-        functools.partial(last_kernel, local_rows * n * second_cells),
+        functools.partial(last_kernel, total_first * second_cells),
         "last",
         (f32(n, depth_own, rank), f32(1, rank)),
         [],

time: 74.6 us -> 76.6 us (1.027)
  starting transfers between devices: 0 us -> 7.46 us
  Pallas kernels: 70.7 us -> 65.4 us
    pallas_call x1, Pallas kernels: 18.5 us -> 11 us  [on_device(): call(functools.partial(second_exchange, n), 'second_exchange', (f32(secon...]
    all_to_all x0 -> x1, starting transfers between devices: none -> 7.46 us  [on_device(): swapped = lax.all_to_all(blocks, 'row', 0, 0, tiled=True)]
    unnamed x10 -> x6, local copies, waits for them, and re-layouts: 2.95 us -> 0.73 us
    pallas_call x2, Pallas kernels: 14.9 us -> 16.9 us  [the longest x1 16.1 us: on_device(): call(first_kernel, 'first', f32(local_rows, rank), split + staged + [pltp...]
    transpose x0 -> x1, local copies, waits for them, and re-layouts: none -> 1.88 us  [on_device(): tensor.reshape(local_rows, n, second_own, depth_cells).transpose(1, 0, 2, 3)]
    pallas_call x1, Pallas kernels: 7.92 us -> 9.2 us  [on_device(): call(functools.partial(third_exchange, n), 'third_exchange', f32(n, depth...]
    pallas_call x1, Pallas kernels: 13.2 us -> 12.2 us  [on_device(): call(functools.partial(first_exchange, n), 'first_exchange', (f32(local_r...]
  transfers between devices with their start and end apart: 0 -> 1, of which waited for: 0 -> 0; matrix products, arithmetic and copies ran while one was open for 0% -> 0% of each run, Pallas kernels for 0% -> 49%
where the time goes in v3:
time: 76.6 us; the launch traced here: 76.2 us
  Pallas kernels  65.4 us (85%)
  starting transfers between devices  7.46 us (10%)
  local copies, waits for them, and re-layouts  2.6 us (3%)
    pallas_call x2, Pallas kernels, solve(): call(solve_kernel, 'solve', (f32(padded, rank), f32(*factor.shape)), [])  16.2 us
    pallas_call x1, Pallas kernels, on_device(): call(first_kernel, 'first', f32(local_rows, rank), split + staged + [pltp...  16.1 us
    pallas_call x1, Pallas kernels, on_device(): call(functools.partial(first_exchange, n), 'first_exchange', (f32(local_r...  12.2 us
    pallas_call x1, Pallas kernels, on_device(): call(functools.partial(second_exchange, n), 'second_exchange', (f32(secon...  11 us
    pallas_call x1, Pallas kernels, on_device(): call(functools.partial(third_exchange, n), 'third_exchange', f32(n, depth...  9.2 us
    all_to_all x1, starting transfers between devices, on_device(): swapped = lax.all_to_all(blocks, 'row', 0, 0, tiled=True)  7.46 us
    transpose x1, local copies, waits for them, and re-layouts, on_device(): tensor.reshape(local_rows, n, second_own, depth_cells).transpose(1, 0, 2, 3)  1.88 us
  transfers between devices with their start and end apart: 1, of which 0 were waited for; matrix products, arithmetic and copies ran while one was open for 0% of the time, Pallas kernels for 49%

profile of v3, /device:TPU:0, one launch (start us, length us, event | category | flops | bytes accessed | tf_op | source)
XLA Modules:
  0.0 76.2 jit_solution(1337234143602989760)
XLA Ops:
  0.6 1.9 %copy_bitcast_fusion = f32[16,8,8,128]{3,2,1,0:T(8,128)} fusion(f32[8,128,128]{2,1,0:T(8,128)} %tensor_ref.1), kind=kLoop, calls=%fused_computation | loop fusion | bytes 1048576 | tf_op jit(solution)/shard_map/transpose | solution.py:339
  2.5 7.5 %all-to-all-start = ((f32[16,8,8,128]{3,2,1,0:T(8,128)}), f32[16,8,8,128]{3,2,1,0:T(8,128)}, u32[]{:S(2)}, u32[]{:S(2)}) async-start(f32[16,8,8,128]{3,2,1,0:T(8,128)} %copy_bitcast_fusion), calls=%async_computation | async-start | bytes 1048576 | tf_op jit(solution)/shard_map/all_to_all | solution.py:340
  10.0 0.0 copy-start
  10.0 0.0 copy-start.1
  10.0 16.1 %first.1.raw_ref = f32[8,512]{1,0:T(8,128)} custom-call(f32[8,128,128]{2,1,0:T(8,128)} %tensor_ref.1, f32[128,512]{1,0:T(8,128)} %second_hbm.1, f32[128,512]{1,0:T(8,128)} %third_ref.1), custom_call_target="tpu_custom_call" | custom-call | tf_op jit(solution)/shard_map/first/pallas_call | solution.py:342
  26.1 0.0 copy-done
  26.1 0.0 copy-done.1
  26.1 0.0 copy-start.2
  26.2 0.7 copy-done.2
  26.9 12.2 %first_exchange.1 = (f32[8,512]{1,0:T(8,128)S(1)}, f32[128,512]{1,0:T(8,128)S(1)}, f32[512,512]{1,0:T(8,128)S(1)}, f32[8,512]{1,0:T(8,128)S(1)}, f32[2,512]{1,0:...) custom-call(f32[8,512]{1,0:T(8,128)S(1)} %copy-done.2, ...), custom_call_target="tpu_custom_call" | custom-call | tf_op jit(solution)/shard_map/first_exchange/pallas_call | solution.py:350
  39.1 8.9 %solve.2 = (f32[8,512]{1,0:T(8,128)S(1)}, f32[8,512]{1,0:T(8,128)}) custom-call(f32[8,512]{1,0:T(8,128)S(1)} %get-tuple-element.24.right_ref, f32[2,512]{1,0:T(2,128)S(1)} %get-tuple-element.25.scales_ref, bf16[512,512]{1,0:T(8,128)(2,1)S(1)} %get-tuple-element.26.vh_ref, bf16[512,512]{1,0:T(8,128)(2,1)S(1)} %get-tuple-element.27.vm_ref, ...), custom_call_target="tpu_custom_call" | custom-call | tf_op jit(solution)/shard_map/solve/pallas_call | solution.py:334
  48.0 0.0 all-to-all-done.swapped_ref
  48.0 11.0 %second_exchange.1 = (f32[8,512]{1,0:T(8,128)S(1)}, f32[8,512]{1,0:T(8,128)S(1)}, f32[2,512]{1,0:T(2,128)S(1)}, bf16[512,512]{1,0:T(8,128)(2,1)S(1)}, bf16[512,5...) custom-call(f32[8,512]{1,0:T(8,128)S(1)} %get-tuple-element.31.raw_ref, f32[16,8,8,128]{3,2,1,0:T(8,128)} %all-to-all-done.swapped_ref, ...), custom_call_target="tpu_custom_call" | custom-call | tf_op jit(solution)/shard_map/second_exchange/pallas_call | solution.py:358
  58.9 7.3 %solve.3 = (f32[8,512]{1,0:T(8,128)S(1)}, f32[8,512]{1,0:T(8,128)}) custom-call(f32[8,512]{1,0:T(8,128)S(1)} %get-tuple-element.34.right_ref, f32[2,512]{1,0:T(2,128)S(1)} %get-tuple-element.35.scales_ref, bf16[512,512]{1,0:T(8,128)(2,1)S(1)} %get-tuple-element.36.vh_ref, bf16[512,512]{1,0:T(8,128)(2,1)S(1)} %get-tuple-element.37.vm_ref, ...), custom_call_target="tpu_custom_call" | custom-call | tf_op jit(solution)/shard_map/solve/pallas_call | solution.py:334
  66.2 9.2 %third_exchange.1.raw_ref = f32[16,8,512]{2,1,0:T(8,128)S(1)} custom-call(f32[8,512]{1,0:T(8,128)S(1)} %get-tuple-element.41.raw_ref), custom_call_target="tpu_custom_call" | custom-call | tf_op jit(solution)/shard_map/third_exchange/pallas_call | solution.py:366
  75.4 0.8 %last.1 = (f32[16,8,512]{2,1,0:T(8,128)}, f32[1,512]{1,0:T(1,128)}) custom-call(f32[16,8,512]{2,1,0:T(8,128)S(1)} %third_exchange.1.raw_ref), custom_call_target="tpu_custom_call" | custom-call | tf_op jit(solution)/shard_map/last/pallas_call | solution.py:373
Async XLA Ops:
  2.5 45.5 %all-to-all-start = ((f32[16,8,8,128]{3,2,1,0:T(8,128)}), f32[16,8,8,128]{3,2,1,0:T(8,128)}, u32[]{:S(2)}, u32[]{:S(2)}) async-start(f32[16,8,8,128]{3,2,1,0:T(8,128)} %copy_bitcast_fusion), calls=%async_computation | async-start | bytes 1048576 | tf_op jit(solution)/shard_map/all_to_all | solution.py:340
  10.0 16.1 %copy-start = (f32[8,128,128]{2,1,0:T(8,128)S(1)}, f32[8,128,128]{2,1,0:T(8,128)}, u32[]{:S(2)}) copy-start(f32[8,128,128]{2,1,0:T(8,128)} %tensor_ref.1) | copy-start | bytes 1572868
  10.0 16.1 %copy-start.1 = (f32[128,512]{1,0:T(8,128)S(1)}, f32[128,512]{1,0:T(8,128)}, u32[]{:S(2)}) copy-start(f32[128,512]{1,0:T(8,128)} %third_ref.1) | copy-start | bytes 786436
  26.1 0.7 copy-start.2

commit v4 on v3

--- a/solution.py
+++ b/solution.py
@@ -245,10 +245,10 @@
     right_ref[...] = scatter_finish(scatters, parts_ref) / scales
     for copy in gathers + scatters:
         copy.wait_send()
-    return factor, own_gram, scales
-
-
-def first_exchange(n, raw_ref, tensor_ref, third_ref, factor_ref, all_factor_ref, gram_ref, *refs):
+    return own_gram, scales
+
+
+def first_exchange(n, raw_ref, tensor_ref, third_ref, factor_ref, gram_ref, *refs):
     place = Place(n)
     wait_barrier = place.greet()
     raw = raw_ref[...]
@@ -257,22 +257,54 @@
     third = third_ref[...]
     pairs = jnp.concatenate([third * raw[i : i + 1] for i in range(local_rows)], axis=0)
     terms = dot(slabs, pairs)
-    factor, gram_a, scales = exchange(place, wait_barrier, terms, gram(third), raw_ref, *refs)
-    all_factor_ref[...] = factor
+    gram_a, scales = exchange(place, wait_barrier, terms, gram(third), raw_ref, *refs)
     gram_ref[...] = gram_a
     factor_ref[...] = raw / scales
 
 
-def second_exchange(n, raw_ref, swapped_ref, first_ref, gram_a_ref, factor_ref, *refs):
+def second_exchange(
+    n, raw_ref, tensor_ref, first_ref, gram_a_ref, factor_ref, right_ref, scales_ref, vh_ref, vm_ref, vl_ref,
+    all_ref, part_ref, pair_ref, parts_ref, gather_sems, forward_sems, scatter_sems, turned_ref
+):
     place = Place(n)
     wait_barrier = place.greet()
-    raw = raw_ref[...]
-    turned = swapped_ref[...].reshape(-1, swapped_ref.shape[-1]).T
+    local_rows, second_cells, depth_cells = tensor_ref.shape
+    wide = second_cells // place.chips
+    for chip in range(place.chips):
+        slab = tensor_ref[:, chip * wide : (chip + 1) * wide, :]
+        turned_ref[chip] = slab.reshape(local_rows * wide, depth_cells).T
     first = first_ref[...]
-    pairs = jnp.concatenate([raw * first[i : i + 1] for i in range(first.shape[0])], axis=0)
-    terms = dot(turned, pairs)
-    _, _, scales = exchange(place, wait_barrier, terms, gram_a_ref[...], raw_ref, *refs)
-    factor_ref[...] = raw / scales
+    wait_barrier()
+    copies = gather_start(place, raw_ref, all_ref, gather_sems)
+
+    def terms_of(step):
+        chip = place.chip_before(step)
+        rows = jnp.concatenate([all_ref[chip * 2], all_ref[chip * 2 + 1]], axis=0)
+        pairs = jnp.concatenate([rows * first[i : i + 1] for i in range(local_rows)], axis=0)
+        return dot(turned_ref[chip], pairs)
+
+    forwards = [copies[-1]]
+    terms = None
+    for step in range(1, place.chips + 1):
+        if step < place.chips:
+            copies[step - 1].wait_recv()
+            slot = all_ref.at[place.chip_before(step) * 2 + place.core]
+            forward = place.send(slot, slot, forward_sems, step, place.partner)
+            forward.start()
+            forwards.append(forward)
+        forwards[step - 1].wait_recv()
+        term = terms_of(step - 1)
+        terms = term if terms is None else terms + term
+    split_parts(place, terms, part_ref)
+    pair_copy = pair_start(place, part_ref, pair_ref, scatter_sems)
+    factor, scales = unit_columns(all_ref[...])
+    factor_ref[...] = raw_ref[...] / scales
+    own_gram = gram(factor)
+    scatters = scatter_start(place, pair_copy, part_ref, pair_ref, parts_ref, scatter_sems)
+    scales_ref[0:1], scales_ref[1:2] = prepare(own_gram, gram_a_ref[...], vh_ref, vm_ref, vl_ref)
+    right_ref[...] = scatter_finish(scatters, parts_ref) / scales
+    for copy in copies[:-1] + forwards + scatters:
+        copy.wait_send()
 
 
 def third_exchange(n, raw_ref, all_out_ref, all_ref, gather_sems, forward_sems):
@@ -336,8 +368,6 @@
         )
         return raw[:rows], out
 
-    blocks = tensor.reshape(local_rows, n, second_own, depth_cells).transpose(1, 0, 2, 3)
-    swapped = lax.all_to_all(blocks, "row", 0, 0, tiled=True)
     staged = [pltpu.VMEM(whole.shape, jnp.float32) for whole in (tensor, init_second, init_third)]
     raw_a = call(
         first_kernel,
@@ -347,10 +377,10 @@
         in_specs=[pl.BlockSpec(memory_space=pltpu.HBM)] * 3,
         limit=FIRST_LIMIT,
     )(tensor, init_second, init_third)
-    factor_first, all_first, gram_a, right_b, scales_b, *parts_b = call(
+    factor_first, gram_a, right_b, scales_b, *parts_b = call(
         functools.partial(first_exchange, n),
         "first_exchange",
-        (f32(local_rows, rank), f32(total_first, rank), f32(rank, rank), f32(second_own, rank), f32(2, rank), *system),
+        (f32(local_rows, rank), f32(rank, rank), f32(second_own, rank), f32(2, rank), *system),
         buffers(local_rows, second_own),
         0,
     )(raw_a, tensor, init_third)
@@ -359,9 +389,10 @@
         functools.partial(second_exchange, n),
         "second_exchange",
         (f32(second_own, rank), f32(depth_own, rank), f32(2, rank), *system),
-        buffers(second_own, depth_own),
+        buffers(second_own, depth_own)
+        + [pltpu.VMEM((chips, depth_cells, local_rows * second_cells // chips), jnp.float32)],
         1,
-    )(raw_b, swapped, all_first, gram_a)
+    )(raw_b, tensor, factor_first, gram_a)
     raw_c, factor_second_out = solve(right_c, scales_c, parts_c, factor_second)
     all_c = call(
         functools.partial(third_exchange, n),

time: 76.6 us -> 73.7 us (0.962)
  starting transfers between devices: 7.46 us -> 0 us
  Pallas kernels: 65.4 us -> 72.1 us
  local copies, waits for them, and re-layouts: 2.6 us -> 0.72 us
    all_to_all x1 -> x0, starting transfers between devices: 7.46 us -> none  [on_device(): swapped = lax.all_to_all(blocks, 'row', 0, 0, tiled=True)]
    pallas_call x1, Pallas kernels: 11 us -> 17.5 us  [on_device(): call(functools.partial(second_exchange, n), 'second_exchange', (f32(secon...]
    transpose x1 -> x0, local copies, waits for them, and re-layouts: 1.88 us -> none  [on_device(): tensor.reshape(local_rows, n, second_own, depth_cells).transpose(1, 0, 2, 3)]
    pallas_call x1, Pallas kernels: 12.2 us -> 13.5 us  [on_device(): call(functools.partial(first_exchange, n), 'first_exchange', (f32(local_r...]
    pallas_call x1, Pallas kernels: 9.2 us -> 8.03 us  [on_device(): call(functools.partial(third_exchange, n), 'third_exchange', f32(n, depth...]
  transfers between devices with their start and end apart: 1 -> 0, of which waited for: 0 -> 0; matrix products, arithmetic and copies ran while one was open for 0% -> 0% of each run, Pallas kernels for 49% -> 0%
where the time goes in v4:
time: 73.7 us; the launch traced here: 73.5 us
  Pallas kernels  72.1 us (98%)
    pallas_call x1, Pallas kernels, on_device(): call(functools.partial(second_exchange, n), 'second_exchange', (f32(secon...  17.5 us
    pallas_call x2, Pallas kernels, solve(): call(solve_kernel, 'solve', (f32(padded, rank), f32(*factor.shape)), [])  16.2 us
    pallas_call x1, Pallas kernels, on_device(): call(first_kernel, 'first', f32(local_rows, rank), split + staged + [pltp...  16.1 us
    pallas_call x1, Pallas kernels, on_device(): call(functools.partial(first_exchange, n), 'first_exchange', (f32(local_r...  13.5 us
    pallas_call x1, Pallas kernels, on_device(): call(functools.partial(third_exchange, n), 'third_exchange', f32(n, depth...  8.03 us

profile of v4, /device:TPU:0, one launch (start us, length us, event | category | flops | bytes accessed | tf_op | source)
XLA Modules:
  0.0 73.5 jit_solution(2846125067789871479)
XLA Ops:
  0.6 0.0 copy-start
  0.6 0.0 copy-start.1
  0.7 16.1 %first.1.raw_ref = f32[8,512]{1,0:T(8,128)} custom-call(f32[8,128,128]{2,1,0:T(8,128)} %tensor_ref.3, f32[128,512]{1,0:T(8,128)} %second_hbm.1, f32[128,512]{1,0:T(8,128)} %third_ref.1), custom_call_target="tpu_custom_call" | custom-call | tf_op jit(solution)/shard_map/first/pallas_call | solution.py:372
  16.8 0.0 copy-done
  16.8 0.0 copy-done.1
  16.8 0.0 copy-start.2
  16.8 0.7 copy-done.2
  17.5 13.5 %first_exchange.1 = (f32[8,512]{1,0:T(8,128)S(1)}, f32[512,512]{1,0:T(8,128)S(1)}, f32[8,512]{1,0:T(8,128)S(1)}, f32[2,512]{1,0:T(2,128)S(1)}, bf16[512,512]{1,0...) custom-call(f32[8,512]{1,0:T(8,128)S(1)} %copy-done.2, f32[8,128,128]{2,1,0:T(8,128)S(1)} %copy-done, ...), custom_call_target="tpu_custom_call" | custom-call | tf_op jit(solution)/shard_map/first_exchange/pallas_call | solution.py:380
  31.0 8.9 %solve.2 = (f32[8,512]{1,0:T(8,128)S(1)}, f32[8,512]{1,0:T(8,128)}) custom-call(f32[8,512]{1,0:T(8,128)S(1)} %get-tuple-element.23.right_ref, f32[2,512]{1,0:T(2,128)S(1)} %get-tuple-element.24.scales_ref, bf16[512,512]{1,0:T(8,128)(2,1)S(1)} %get-tuple-element.25.vh_ref, bf16[512,512]{1,0:T(8,128)(2,1)S(1)} %get-tuple-element.26.vm_ref, ...), custom_call_target="tpu_custom_call" | custom-call | tf_op jit(solution)/shard_map/solve/pallas_call | solution.py:366
  39.9 17.5 %second_exchange.1 = (f32[8,512]{1,0:T(8,128)S(1)}, f32[8,512]{1,0:T(8,128)S(1)}, f32[2,512]{1,0:T(2,128)S(1)}, bf16[512,512]{1,0:T(8,128)(2,1)S(1)}, bf16[512,5...) custom-call(f32[8,512]{1,0:T(8,128)S(1)} %get-tuple-element.30.raw_ref, f32[8,128,128]{2,1,0:T(8,128)S(1)} %copy-done, ...), custom_call_target="tpu_custom_call" | custom-call | tf_op jit(solution)/shard_map/second_exchange/pallas_call | solution.py:388
  57.4 7.3 %solve.3 = (f32[8,512]{1,0:T(8,128)S(1)}, f32[8,512]{1,0:T(8,128)}) custom-call(f32[8,512]{1,0:T(8,128)S(1)} %get-tuple-element.32.right_ref, f32[2,512]{1,0:T(2,128)S(1)} %get-tuple-element.33.scales_ref, bf16[512,512]{1,0:T(8,128)(2,1)S(1)} %get-tuple-element.34.vh_ref, bf16[512,512]{1,0:T(8,128)(2,1)S(1)} %get-tuple-element.35.vm_ref, ...), custom_call_target="tpu_custom_call" | custom-call | tf_op jit(solution)/shard_map/solve/pallas_call | solution.py:366
  64.7 8.0 %third_exchange.1.raw_ref = f32[16,8,512]{2,1,0:T(8,128)S(1)} custom-call(f32[8,512]{1,0:T(8,128)S(1)} %get-tuple-element.39.raw_ref), custom_call_target="tpu_custom_call" | custom-call | tf_op jit(solution)/shard_map/third_exchange/pallas_call | solution.py:397
  72.7 0.8 %last.1 = (f32[16,8,512]{2,1,0:T(8,128)}, f32[1,512]{1,0:T(1,128)}) custom-call(f32[16,8,512]{2,1,0:T(8,128)S(1)} %third_exchange.1.raw_ref), custom_call_target="tpu_custom_call" | custom-call | tf_op jit(solution)/shard_map/last/pallas_call | solution.py:404
Async XLA Ops:
  0.6 16.1 %copy-start = (f32[8,128,128]{2,1,0:T(8,128)S(1)}, f32[8,128,128]{2,1,0:T(8,128)}, u32[]{:S(2)}) copy-start(f32[8,128,128]{2,1,0:T(8,128)} %tensor_ref.3) | copy-start | bytes 1572868
  0.6 16.1 %copy-start.1 = (f32[128,512]{1,0:T(8,128)S(1)}, f32[128,512]{1,0:T(8,128)}, u32[]{:S(2)}) copy-start(f32[128,512]{1,0:T(8,128)} %third_ref.1) | copy-start | bytes 786436
  16.8 0.7 copy-start.2

commit v5 on v4

--- a/solution.py
+++ b/solution.py
@@ -15,6 +15,7 @@
 SOLVE_TOL = 4e-06
 MAX_ROUNDS = 2048
 UNROLL = 3
+TINY = 1e-30
 VMEM_LIMIT = 40 * 1024 * 1024
 FIRST_LIMIT = 63 * 1024 * 1024
 
@@ -62,30 +63,32 @@
     def row_sum(value):
         return jnp.sum(value, axis=1, keepdims=True)
 
-    def one(x, r, p, rz):
-        q = apply(p)
-        curvature = row_sum(p * q)
-        alpha = jnp.where(curvature > 0, rz / curvature, 0.0)
-        x = x + alpha * p
-        r = r - alpha * q
+    def one(x, r, p, q, rz, alpha):
         z = r * precondition
+        w = apply(z)
         rz_next = row_sum(r * z)
+        curvature = row_sum(w * z)
         beta = jnp.where(rz > 0, rz_next / rz, 0.0)
-        return x, r, z + beta * p, rz_next
+        curvature = curvature - beta * rz_next / alpha
+        alpha = jnp.where(curvature > 0, rz_next / curvature, TINY)
+        p = z + beta * p
+        q = w + beta * q
+        return x + alpha * p, r - alpha * q, p, q, rz_next, alpha
 
     def body(carry):
-        count, _, x, r, p, rz = carry
+        count, _, *state = carry
         for _ in range(UNROLL):
-            x, r, p, rz = one(x, r, p, rz)
+            state = one(*state)
+        x, r = state[:2]
         excess = row_sum(r * r) - (SOLVE_TOL * RIDGE) ** 2 * row_sum(x * x)
-        return count + 1, jnp.max(excess), x, r, p, rz
+        return count + 1, jnp.max(excess), *state
 
     def unfinished(carry):
         return jnp.logical_and(carry[1] > 0, carry[0] < MAX_ROUNDS)
 
     r = right / largest
-    z = r * precondition
-    start = (jnp.int32(0), jnp.float32(1.0), jnp.zeros_like(r), r, z, row_sum(r * z))
+    zero = jnp.zeros_like(r)
+    start = (jnp.int32(0), jnp.float32(1.0), zero, r, zero, zero, jnp.zeros_like(largest), jnp.ones_like(largest))
     x = lax.while_loop(unfinished, body, start)[2]
     return x * (largest * inverse_mean)
 

time: 73.7 us -> 71.2 us (0.966)
  Pallas kernels: 72.1 us -> 69.5 us
    pallas_call x2, Pallas kernels: 16.2 us -> 14.6 us  [solve(): call(solve_kernel, 'solve', (f32(padded, rank), f32(*factor.shape)), [])]
    pallas_call x1, Pallas kernels: 16.1 us -> 15.1 us  [on_device(): call(first_kernel, 'first', f32(local_rows, rank), split + staged + [pltp...]
where the time goes in v5:
time: 71.2 us; the launch traced here: 70.9 us
  Pallas kernels  69.5 us (98%)
  local copies, waits for them, and re-layouts  0.72 us (1%)
    pallas_call x1, Pallas kernels, on_device(): call(functools.partial(second_exchange, n), 'second_exchange', (f32(secon...  17.5 us
    pallas_call x1, Pallas kernels, on_device(): call(first_kernel, 'first', f32(local_rows, rank), split + staged + [pltp...  15.1 us
    pallas_call x2, Pallas kernels, solve(): call(solve_kernel, 'solve', (f32(padded, rank), f32(*factor.shape)), [])  14.6 us
    pallas_call x1, Pallas kernels, on_device(): call(functools.partial(first_exchange, n), 'first_exchange', (f32(local_r...  13.5 us
    pallas_call x1, Pallas kernels, on_device(): call(functools.partial(third_exchange, n), 'third_exchange', f32(n, depth...  8.03 us

profile of v5, /device:TPU:0, one launch (start us, length us, event | category | flops | bytes accessed | tf_op | source)
XLA Modules:
  0.0 70.9 jit_solution(5520516667892803821)
XLA Ops:
  0.6 0.0 copy-start
  0.6 0.0 copy-start.1
  0.7 15.1 %first.1.raw_ref = f32[8,512]{1,0:T(8,128)} custom-call(f32[8,128,128]{2,1,0:T(8,128)} %tensor_ref.3, f32[128,512]{1,0:T(8,128)} %second_hbm.1, f32[128,512]{1,0:T(8,128)} %third_ref.1), custom_call_target="tpu_custom_call" | custom-call | tf_op jit(solution)/shard_map/first/pallas_call | solution.py:375
  15.8 0.0 copy-done
  15.8 0.0 copy-done.1
  15.8 0.0 copy-start.2
  15.8 0.7 copy-done.2
  16.5 13.5 %first_exchange.1 = (f32[8,512]{1,0:T(8,128)S(1)}, f32[512,512]{1,0:T(8,128)S(1)}, f32[8,512]{1,0:T(8,128)S(1)}, f32[2,512]{1,0:T(2,128)S(1)}, bf16[512,512]{1,0...) custom-call(f32[8,512]{1,0:T(8,128)S(1)} %copy-done.2, f32[8,128,128]{2,1,0:T(8,128)S(1)} %copy-done, ...), custom_call_target="tpu_custom_call" | custom-call | tf_op jit(solution)/shard_map/first_exchange/pallas_call | solution.py:383
  30.0 8.0 %solve.2 = (f32[8,512]{1,0:T(8,128)S(1)}, f32[8,512]{1,0:T(8,128)}) custom-call(f32[8,512]{1,0:T(8,128)S(1)} %get-tuple-element.23.right_ref, f32[2,512]{1,0:T(2,128)S(1)} %get-tuple-element.24.scales_ref, bf16[512,512]{1,0:T(8,128)(2,1)S(1)} %get-tuple-element.25.vh_ref, bf16[512,512]{1,0:T(8,128)(2,1)S(1)} %get-tuple-element.26.vm_ref, ...), custom_call_target="tpu_custom_call" | custom-call | tf_op jit(solution)/shard_map/solve/pallas_call | solution.py:369
  38.0 17.5 %second_exchange.1 = (f32[8,512]{1,0:T(8,128)S(1)}, f32[8,512]{1,0:T(8,128)S(1)}, f32[2,512]{1,0:T(2,128)S(1)}, bf16[512,512]{1,0:T(8,128)(2,1)S(1)}, bf16[512,5...) custom-call(f32[8,512]{1,0:T(8,128)S(1)} %get-tuple-element.30.raw_ref, f32[8,128,128]{2,1,0:T(8,128)S(1)} %copy-done, ...), custom_call_target="tpu_custom_call" | custom-call | tf_op jit(solution)/shard_map/second_exchange/pallas_call | solution.py:391
  55.5 6.6 %solve.3 = (f32[8,512]{1,0:T(8,128)S(1)}, f32[8,512]{1,0:T(8,128)}) custom-call(f32[8,512]{1,0:T(8,128)S(1)} %get-tuple-element.32.right_ref, f32[2,512]{1,0:T(2,128)S(1)} %get-tuple-element.33.scales_ref, bf16[512,512]{1,0:T(8,128)(2,1)S(1)} %get-tuple-element.34.vh_ref, bf16[512,512]{1,0:T(8,128)(2,1)S(1)} %get-tuple-element.35.vm_ref, ...), custom_call_target="tpu_custom_call" | custom-call | tf_op jit(solution)/shard_map/solve/pallas_call | solution.py:369
  62.1 8.0 %third_exchange.1.raw_ref = f32[16,8,512]{2,1,0:T(8,128)S(1)} custom-call(f32[8,512]{1,0:T(8,128)S(1)} %get-tuple-element.39.raw_ref), custom_call_target="tpu_custom_call" | custom-call | tf_op jit(solution)/shard_map/third_exchange/pallas_call | solution.py:400
  70.1 0.8 %last.1 = (f32[16,8,512]{2,1,0:T(8,128)}, f32[1,512]{1,0:T(1,128)}) custom-call(f32[16,8,512]{2,1,0:T(8,128)S(1)} %third_exchange.1.raw_ref), custom_call_target="tpu_custom_call" | custom-call | tf_op jit(solution)/shard_map/last/pallas_call | solution.py:407
Async XLA Ops:
  0.6 15.2 %copy-start = (f32[8,128,128]{2,1,0:T(8,128)S(1)}, f32[8,128,128]{2,1,0:T(8,128)}, u32[]{:S(2)}) copy-start(f32[8,128,128]{2,1,0:T(8,128)} %tensor_ref.3) | copy-start | bytes 1572868
  0.6 15.2 %copy-start.1 = (f32[128,512]{1,0:T(8,128)S(1)}, f32[128,512]{1,0:T(8,128)}, u32[]{:S(2)}) copy-start(f32[128,512]{1,0:T(8,128)} %third_ref.1) | copy-start | bytes 786436
  15.8 0.7 %copy-start.2 = (f32[8,512]{1,0:T(8,128)S(1)}, f32[8,512]{1,0:T(8,128)}, u32[]{:S(2)}) copy-start(f32[8,512]{1,0:T(8,128)} %first.1.raw_ref) | copy-start | bytes 49156

commit v6 on v5

--- a/solution.py
+++ b/solution.py
@@ -302,8 +302,8 @@
     pair_copy = pair_start(place, part_ref, pair_ref, scatter_sems)
     factor, scales = unit_columns(all_ref[...])
     factor_ref[...] = raw_ref[...] / scales
+    scatters = scatter_start(place, pair_copy, part_ref, pair_ref, parts_ref, scatter_sems)
     own_gram = gram(factor)
-    scatters = scatter_start(place, pair_copy, part_ref, pair_ref, parts_ref, scatter_sems)
     scales_ref[0:1], scales_ref[1:2] = prepare(own_gram, gram_a_ref[...], vh_ref, vm_ref, vl_ref)
     right_ref[...] = scatter_finish(scatters, parts_ref) / scales
     for copy in copies[:-1] + forwards + scatters:

time: 71.2 us -> 71.9 us (level)
    pallas_call x1, Pallas kernels: 17.5 us -> 18.3 us  [on_device(): call(functools.partial(second_exchange, n), 'second_exchange', (f32(secon...]
where the time goes in v6:
time: 71.9 us; the launch traced here: 71.6 us
  Pallas kernels  70.2 us (98%)
  local copies, waits for them, and re-layouts  0.72 us (1%)
    pallas_call x1, Pallas kernels, on_device(): call(functools.partial(second_exchange, n), 'second_exchange', (f32(secon...  18.3 us
    pallas_call x1, Pallas kernels, on_device(): call(first_kernel, 'first', f32(local_rows, rank), split + staged + [pltp...  15.1 us
    pallas_call x2, Pallas kernels, solve(): call(solve_kernel, 'solve', (f32(padded, rank), f32(*factor.shape)), [])  14.6 us
    pallas_call x1, Pallas kernels, on_device(): call(functools.partial(first_exchange, n), 'first_exchange', (f32(local_r...  13.5 us
    pallas_call x1, Pallas kernels, on_device(): call(functools.partial(third_exchange, n), 'third_exchange', f32(n, depth...  7.97 us

profile of v6, /device:TPU:0, one launch (start us, length us, event | category | flops | bytes accessed | tf_op | source)
XLA Modules:
  0.0 71.6 jit_solution(7098891303172423517)
XLA Ops:
  0.6 0.0 copy-start
  0.6 0.0 copy-start.1
  0.7 15.1 %first.1.raw_ref = f32[8,512]{1,0:T(8,128)} custom-call(f32[8,128,128]{2,1,0:T(8,128)} %tensor_ref.3, f32[128,512]{1,0:T(8,128)} %second_hbm.1, f32[128,512]{1,0:T(8,128)} %third_ref.1), custom_call_target="tpu_custom_call" | custom-call | tf_op jit(solution)/shard_map/first/pallas_call | solution.py:375
  15.8 0.0 copy-done
  15.8 0.0 copy-done.1
  15.8 0.0 copy-start.2
  15.8 0.7 copy-done.2
  16.5 13.5 %first_exchange.1 = (f32[8,512]{1,0:T(8,128)S(1)}, f32[512,512]{1,0:T(8,128)S(1)}, f32[8,512]{1,0:T(8,128)S(1)}, f32[2,512]{1,0:T(2,128)S(1)}, bf16[512,512]{1,0...) custom-call(f32[8,512]{1,0:T(8,128)S(1)} %copy-done.2, f32[8,128,128]{2,1,0:T(8,128)S(1)} %copy-done, ...), custom_call_target="tpu_custom_call" | custom-call | tf_op jit(solution)/shard_map/first_exchange/pallas_call | solution.py:383
  30.0 8.0 %solve.2 = (f32[8,512]{1,0:T(8,128)S(1)}, f32[8,512]{1,0:T(8,128)}) custom-call(f32[8,512]{1,0:T(8,128)S(1)} %get-tuple-element.23.right_ref, f32[2,512]{1,0:T(2,128)S(1)} %get-tuple-element.24.scales_ref, bf16[512,512]{1,0:T(8,128)(2,1)S(1)} %get-tuple-element.25.vh_ref, bf16[512,512]{1,0:T(8,128)(2,1)S(1)} %get-tuple-element.26.vm_ref, ...), custom_call_target="tpu_custom_call" | custom-call | tf_op jit(solution)/shard_map/solve/pallas_call | solution.py:369
  38.0 18.3 %second_exchange.1 = (f32[8,512]{1,0:T(8,128)S(1)}, f32[8,512]{1,0:T(8,128)S(1)}, f32[2,512]{1,0:T(2,128)S(1)}, bf16[512,512]{1,0:T(8,128)(2,1)S(1)}, bf16[512,5...) custom-call(f32[8,512]{1,0:T(8,128)S(1)} %get-tuple-element.30.raw_ref, f32[8,128,128]{2,1,0:T(8,128)S(1)} %copy-done, ...), custom_call_target="tpu_custom_call" | custom-call | tf_op jit(solution)/shard_map/second_exchange/pallas_call | solution.py:391
  56.3 6.6 %solve.3 = (f32[8,512]{1,0:T(8,128)S(1)}, f32[8,512]{1,0:T(8,128)}) custom-call(f32[8,512]{1,0:T(8,128)S(1)} %get-tuple-element.32.right_ref, f32[2,512]{1,0:T(2,128)S(1)} %get-tuple-element.33.scales_ref, bf16[512,512]{1,0:T(8,128)(2,1)S(1)} %get-tuple-element.34.vh_ref, bf16[512,512]{1,0:T(8,128)(2,1)S(1)} %get-tuple-element.35.vm_ref, ...), custom_call_target="tpu_custom_call" | custom-call | tf_op jit(solution)/shard_map/solve/pallas_call | solution.py:369
  62.9 8.0 %third_exchange.1.raw_ref = f32[16,8,512]{2,1,0:T(8,128)S(1)} custom-call(f32[8,512]{1,0:T(8,128)S(1)} %get-tuple-element.39.raw_ref), custom_call_target="tpu_custom_call" | custom-call | tf_op jit(solution)/shard_map/third_exchange/pallas_call | solution.py:400
  70.8 0.8 %last.1 = (f32[16,8,512]{2,1,0:T(8,128)}, f32[1,512]{1,0:T(1,128)}) custom-call(f32[16,8,512]{2,1,0:T(8,128)S(1)} %third_exchange.1.raw_ref), custom_call_target="tpu_custom_call" | custom-call | tf_op jit(solution)/shard_map/last/pallas_call | solution.py:407
Async XLA Ops:
  0.6 15.2 %copy-start = (f32[8,128,128]{2,1,0:T(8,128)S(1)}, f32[8,128,128]{2,1,0:T(8,128)}, u32[]{:S(2)}) copy-start(f32[8,128,128]{2,1,0:T(8,128)} %tensor_ref.3) | copy-start | bytes 1572868
  0.6 15.2 %copy-start.1 = (f32[128,512]{1,0:T(8,128)S(1)}, f32[128,512]{1,0:T(8,128)}, u32[]{:S(2)}) copy-start(f32[128,512]{1,0:T(8,128)} %third_ref.1) | copy-start | bytes 786436
  15.8 0.7 %copy-start.2 = (f32[8,512]{1,0:T(8,128)S(1)}, f32[8,512]{1,0:T(8,128)}, u32[]{:S(2)}) copy-start(f32[8,512]{1,0:T(8,128)} %first.1.raw_ref) | copy-start | bytes 49156
